TPU v7x, 512 devices: a whole 4x4x16 slice. The times are simulated.
512 devices in a mesh: seq: 64 (over z, x), tp: 8 (over y, core).
Axes of the slice: x: 4, y: 4, z: 16, core: 2. Of those that a mesh axis runs over, the one named last changes fastest.
Arguments:
- cache_keys: bfloat16 [131072, 2048], P('seq', 'tp'), may hold values from -13 to 13
- cache_values: bfloat16 [131072, 2048], P('seq', 'tp'), may hold values from -12 to 12
- keep_flags: int32 [131072], P('seq'), may hold values from 0 to 1, as said below
- drop_weight: int32 [131072], P('seq'), may hold values from 1 to 255
- req_blocks: int32 [48], replicated, may hold values from 1 to 128, 1024 in all
- queries: bfloat16 [48, 2048], P(None, 'tp'), may hold values from -48 to 48
- new_keys: bfloat16 [48, 2048], P(None, 'tp'), may hold values from -12 to 12
- new_values: bfloat16 [48, 2048], P(None, 'tp'), may hold values from -12 to 12
- out_weight: bfloat16 [2048, 2048], P('tp', 'seq'), may hold values from -0.125 to 0.125
Outputs:
- packed_keys: bfloat16 [66560, 2048], P('seq', 'tp')
- packed_values: bfloat16 [66560, 2048], P('seq', 'tp')
- packed_bias: bfloat16 [66560], P('seq')
- packed_request: int32 [66560], P('seq')
- layer_output: bfloat16 [48, 2048], P('tp', 'seq')
Inputs may be any that keep to these rules, and one draw needn't show every extreme that they name: `keep_flags`: every aligned block of 128 rows keeps between 32 and 64 rows; in every draw all blocks of the rows of some one index of seq keep exactly 64. `req_blocks`: the entries sum to 1024; the largest is 128.
All inputs are finite; a program needn't handle non-finite values.
Results may differ from a plain program's by a relative error of at most 0.009.
Values may be sent and summed in bfloat16 or wider, within the bound.
A program may use at most 64 MiB of HBM per device.

v0:
```python
import jax
import jax.numpy as jnp
from jax import lax
from jax.sharding import PartitionSpec as P

HD = 256
BLOCK = 128
K_DEV = 1040


def shortened(shard):
    return jax.tree.map(lambda a: a.astype(jnp.bfloat16) if a.dtype == jnp.float32 else a, shard)


def local_softmax(queries, keys, values, bias, owner):
    req_count = queries.shape[0]
    heads = queries.shape[1] // HD
    score_scale = 1.0 / jnp.sqrt(jnp.float32(HD))
    query_heads = queries.reshape(req_count, heads, HD)
    key_heads = keys.reshape(keys.shape[0], heads, HD)
    value_heads = values.reshape(values.shape[0], heads, HD)
    scores = (
        jnp.einsum("rhd,ehd->hre", query_heads, key_heads, preferred_element_type=jnp.float32)
        * score_scale
    )
    scores = scores + bias.astype(jnp.float32)[None, None, :]
    member = (owner[None, :] == jnp.arange(req_count, dtype=jnp.int32)[:, None])[None, :, :]
    scores = jnp.where(member, scores, jnp.float32(-1e30))
    peak_score = jnp.max(scores, axis=2)
    probs = jnp.where(member, jnp.exp(scores - peak_score[:, :, None]), jnp.float32(0.0))
    softmax_total = jnp.sum(probs, axis=2)
    weighted = jnp.einsum(
        "hre,ehd->hrd", probs.astype(jnp.bfloat16), value_heads, preferred_element_type=jnp.float32
    )
    return (peak_score, softmax_total, weighted)


def repack(entries, counts, my_index, slot_count):
    seq_count = counts.shape[0]
    peer_slots = (slot_count + seq_count - 1) // seq_count
    all_starts = jnp.cumsum(counts) - counts
    offset = all_starts[my_index]
    local_total = counts[my_index]
    entry_index = jnp.arange(slot_count, dtype=jnp.int32)
    send_flat = jnp.where(
        entry_index < local_total,
        (offset + entry_index) % seq_count * peer_slots + entry_index // seq_count,
        seq_count * peer_slots,
    )

    def pack_peers(array):
        buffer = (
            jnp.zeros((seq_count * peer_slots,) + array.shape[1:], array.dtype)
            .at[send_flat]
            .set(array, mode="drop")
        )
        return buffer.reshape((seq_count, peer_slots) + array.shape[1:])

    received = lax.all_to_all(
        shortened(tuple((pack_peers(item) for item in entries))),
        "seq",
        split_axis=0,
        concat_axis=0,
        tiled=True,
    )
    lead_offset = (my_index - all_starts) % seq_count
    within_source = (
        lead_offset[:, None] + seq_count * jnp.arange(peer_slots, dtype=jnp.int32)[None, :]
    )
    is_valid = within_source < counts[:, None]
    global_rank = all_starts[:, None] + within_source
    target = jnp.where(is_valid, global_rank // seq_count, slot_count).reshape(-1)

    def unpack_peers(array, fill_value):
        flat = array.reshape((seq_count * peer_slots,) + array.shape[2:])
        return (
            jnp.full((slot_count,) + array.shape[2:], fill_value, array.dtype)
            .at[target]
            .set(flat, mode="drop")
        )

    packed_keys = unpack_peers(received[0], 0.0)
    packed_values = unpack_peers(received[1], 0.0)
    packed_bias = unpack_peers(received[2], 0.0)
    packed_request = unpack_peers(received[3], -1.0).astype(jnp.int32)
    return (packed_keys, packed_values, packed_bias, packed_request)


def on_device(
    cache_keys,
    cache_values,
    keep_flags,
    drop_weight,
    req_blocks,
    queries,
    new_keys,
    new_values,
    out_weight,
):
    my_index = lax.axis_index("seq")
    row_count, features = cache_keys.shape
    block_count = row_count // BLOCK
    keep_blocks = keep_flags.reshape(block_count, BLOCK)
    kept_count = jnp.sum(keep_blocks, axis=1)
    within = jnp.cumsum(keep_blocks, axis=1) - keep_blocks
    block_size = kept_count + 1
    block_base = jnp.cumsum(block_size) - block_size
    local_total = jnp.sum(block_size)
    request_ends = jnp.cumsum(req_blocks)
    global_block = my_index * block_count + jnp.arange(block_count, dtype=jnp.int32)
    block_request = jnp.sum(
        (global_block[:, None] >= request_ends[None, :]).astype(jnp.int32), axis=1
    )
    dropped = (drop_weight * (1 - keep_flags)).reshape(block_count, BLOCK)
    fold_weights = dropped.astype(jnp.bfloat16)
    denominator = jnp.sum(dropped.astype(jnp.float32), axis=1)

    def fold_block(cache):
        summed = jnp.einsum(
            "bi,bid->bd",
            fold_weights,
            cache.reshape(block_count, BLOCK, features),
            preferred_element_type=jnp.float32,
        )
        return (summed / denominator[:, None]).astype(jnp.bfloat16)

    folded_keys = fold_block(cache_keys)
    folded_values = fold_block(cache_values)
    folded_bias = jnp.log((BLOCK - kept_count).astype(jnp.float32)).astype(jnp.bfloat16)
    slot_count = K_DEV
    entry_rows = jnp.where(keep_flags == 1, (block_base[:, None] + within).reshape(-1), slot_count)
    fold_entry = block_base + kept_count
    entry_keys = (
        jnp.zeros((slot_count, features), jnp.bfloat16)
        .at[entry_rows]
        .set(cache_keys, mode="drop")
        .at[fold_entry]
        .set(folded_keys)
    )
    entry_values = (
        jnp.zeros((slot_count, features), jnp.bfloat16)
        .at[entry_rows]
        .set(cache_values, mode="drop")
        .at[fold_entry]
        .set(folded_values)
    )
    entry_bias = jnp.zeros((slot_count,), jnp.bfloat16).at[fold_entry].set(folded_bias)
    entry_request = (
        jnp.full((slot_count,), -1, jnp.int32)
        .at[entry_rows]
        .set(jnp.repeat(block_request, BLOCK), mode="drop")
        .at[fold_entry]
        .set(block_request)
    )
    counts = lax.all_gather(local_total.reshape(1), "seq", axis=0, tiled=True)
    entries = (entry_keys, entry_values, entry_bias, entry_request.astype(jnp.bfloat16))
    packed_keys, packed_values, packed_bias, packed_request = repack(
        entries, counts, my_index, slot_count
    )
    softmax_parts = local_softmax(queries, packed_keys, packed_values, packed_bias, packed_request)
    peak_score = lax.pmax(softmax_parts[0], "seq")
    rescale = jnp.exp(softmax_parts[0] - peak_score)
    softmax_total, weighted = lax.psum(
        (softmax_parts[1] * rescale, softmax_parts[2] * rescale[:, :, None]), "seq"
    )
    req_count = queries.shape[0]
    heads = queries.shape[1] // HD
    score_scale = 1.0 / jnp.sqrt(jnp.float32(HD))
    query_heads = queries.reshape(req_count, heads, HD)
    own_score = (
        jnp.einsum(
            "rhd,rhd->hr",
            query_heads,
            new_keys.reshape(req_count, heads, HD),
            preferred_element_type=jnp.float32,
        )
        * score_scale
    )
    final_peak = jnp.maximum(peak_score, own_score)
    rescale_old = jnp.exp(peak_score - final_peak)
    own_prob = jnp.exp(own_score - final_peak)
    new_value_heads = jnp.transpose(new_values.reshape(req_count, heads, HD), (1, 0, 2)).astype(
        jnp.float32
    )
    softmax_total = softmax_total * rescale_old + own_prob
    weighted = weighted * rescale_old[:, :, None] + own_prob[:, :, None] * new_value_heads
    attention_heads = weighted / softmax_total[:, :, None]
    attention = (
        jnp.transpose(attention_heads, (1, 0, 2))
        .reshape(req_count, heads * HD)
        .astype(jnp.bfloat16)
    )
    partial_output = jnp.dot(attention, out_weight, preferred_element_type=jnp.float32)
    layer_output = lax.psum_scatter(partial_output, "tp", scatter_dimension=0, tiled=True).astype(
        jnp.bfloat16
    )
    return (packed_keys, packed_values, packed_bias, packed_request, layer_output)


def solution(mesh):
    in_specs = (
        P("seq", "tp"),
        P("seq", "tp"),
        P("seq"),
        P("seq"),
        P(),
        P(None, "tp"),
        P(None, "tp"),
        P(None, "tp"),
        P("tp", "seq"),
    )
    out_specs = (P("seq", "tp"), P("seq", "tp"), P("seq"), P("seq"), P("tp", "seq"))
    return jax.shard_map(
        on_device, mesh=mesh, in_specs=in_specs, out_specs=out_specs, check_vma=False
    )
```

profile of v0, /device:TPU:1, one launch (start us, length us, event | category | flops | bytes accessed | tf_op | source)
XLA Modules:
  0.0 669.8 jit_solution(16417252213146654245)
XLA Ops:
  0.7 0.8 bitcast_reduce_fusion.1
  1.5 0.1 copy.29
  1.6 0.1 fusion.34
  1.7 0.6 add_subtract_fusion
  2.4 1.3 dynamic-slice
  3.6 1.4 dynamic-update-slice
  5.0 29.6 %all-reduce = s32[64]{0:T(128)S(1)} all-reduce(s32[64]{0:T(128)S(1)} %dynamic-update-slice), channel_id=1, replica_groups=mesh['seq'=64,'tp'=8] {'seq'}, use_global_device_ids=true, to_apply=%add | all-reduce | flops 64 | bytes 512
  34.6 0.1 copy.28
  34.7 0.1 reduce-window.22
  34.8 0.1 reduce.5
  35.0 0.6 dynamic_slice.6
  35.5 0.6 dynamic_slice.7
  36.1 1.3 fusion.44
  37.5 0.7 scatter_custom_fusion.8
  38.2 12.6 %scatter_custom_fusion.9 = bf16[1088]{0:T(1024)(128)(2,1)S(1)} fusion(s32[1040]{0:T(1024)S(1)} %fusion.44, bf16[1040]{0:T(1024)(128)(2,1)S(1)} %scatter_custom_fusion.8, bf16[]{:T(256)} %constant.49.clone.1), kind=kCustom, calls=%fused_computation.101 | custom fusion | bytes 2178 | tf_op jit(solution)/shard_map/scatter | solution.py:55
  50.8 0.8 all_to_all.24
  51.6 7.6 %all-to-all-start.2 = ((bf16[64,1,17]{2,1,0:T(2,128)(2,1)}), bf16[64,1,17]{2,1,0:T(2,128)(2,1)S(1)}, u32[]{:S(2)}, u32[]{:S(2)}) async-start(bf16[64,1,17]{2,1,0:T(2,128)(2,1)} %all_to_all.24), calls=%async_computation.2 | async-start | bytes 65536 | tf_op jit(solution)/shard_map/all_to_all | solution.py:59
  59.2 0.3 reduce_window_sum.34
  59.5 0.7 copy-done.10
  60.1 0.1 copy.32
  60.3 0.1 reduce.11
  60.4 0.6 copy-done.7
  61.1 1.5 fusion.41
  62.5 0.2 convert_reduce_fusion
  62.8 8.1 %scatter_custom_fusion.11 = s32[1040]{0:T(1024)S(1)} fusion(s32[2048]{0:T(1024)S(1)} %get-tuple-element.12, s32[2048]{0:T(1024)S(1)} %broadcast_bitcast_fusion, s32[]{:T(128)} %constant.93.clone.1), kind=kCustom, calls=%fused_computation.91 | custom fusion | bytes 4164 | tf_op jit(solution)/shard_map/scatter | solution.py:151
  70.9 0.8 scatter_fusion
  71.7 12.6 %scatter_custom_fusion.13 = bf16[1088]{0:T(1024)(128)(2,1)S(1)} fusion(s32[1040]{0:T(1024)S(1)} %fusion.44, bf16[1040]{0:T(1024)(128)(2,1)S(1)} %convert_element_type.62, bf16[]{:T(256)} %constant.49.clone.1), kind=kCustom, calls=%fused_computation.99 | custom fusion | bytes 2178 | tf_op jit(solution)/shard_map/scatter | solution.py:55
  84.4 0.8 all_to_all.25
  85.1 14.5 %all-to-all-start.3 = ((bf16[64,1,17]{2,1,0:T(2,128)(2,1)}), bf16[64,1,17]{2,1,0:T(2,128)(2,1)S(1)}, u32[]{:S(2)}, u32[]{:S(2)}) async-start(bf16[64,1,17]{2,1,0:T(2,128)(2,1)} %all_to_all.25), calls=%async_computation.3 | async-start | bytes 65536 | tf_op jit(solution)/shard_map/all_to_all | solution.py:59
  99.7 0.1 bitcast_reduce_fusion
  99.8 9.7 %scatter_custom_fusion = bf16[1040,256]{1,0:T(8,128)(2,1)S(1)} fusion(s32[2048]{0:T(1024)S(1)} %get-tuple-element.12, bf16[2048,256]{1,0:T(8,128)(2,1)} %param.9, bf16[]{:T(256)} %constant.49.clone.1), kind=kCustom, calls=%fused_computation.31 | custom fusion | bytes 532992 | tf_op jit(solution)/shard_map/scatter | solution.py:136
  109.5 1.0 scatter_custom_fusion.1
  110.5 7.9 %scatter_custom_fusion.2 = bf16[1088,256]{1,0:T(8,128)(2,1)S(1)} fusion(s32[1040]{0:T(1024)S(1)} %fusion.44, bf16[1040,256]{1,0:T(8,128)(2,1)S(1)} %scatter_custom_fusion.1, bf16[]{:T(256)} %constant.49.clone.1), kind=kCustom, calls=%fused_computation.23 | custom fusion | bytes 557058 | tf_op jit(solution)/shard_map/scatter | solution.py:55
  118.4 1.1 reshape.417
  119.5 14.7 %all-to-all-start = ((bf16[64,17,256]{2,1,0:T(8,128)(2,1)}), bf16[64,17,256]{2,1,0:T(8,128)(2,1)S(1)}, u32[]{:S(2)}, u32[]{:S(2)}) async-start(bf16[64,17,256]{2,1,0:T(8,128)(2,1)} %reshape.417), calls=%async_computation | async-start | bytes 1572864 | tf_op jit(solution)/shard_map/all_to_all | solution.py:59
  134.2 9.3 %scatter_custom_fusion.4 = bf16[1040,256]{1,0:T(8,128)(2,1)S(1)} fusion(s32[2048]{0:T(1024)S(1)} %get-tuple-element.12, bf16[2048,256]{1,0:T(8,128)(2,1)S(1)} %copy-done.3, bf16[]{:T(256)} %constant.49.clone.1), kind=kCustom, calls=%fused_computation.27 | custom fusion | bytes 532482 | tf_op jit(solution)/shard_map/scatter | solution.py:143
  143.5 0.2 fusion.39
  143.8 1.0 scatter_custom_fusion.5
  144.8 7.9 %scatter_custom_fusion.6 = bf16[1088,256]{1,0:T(8,128)(2,1)S(1)} fusion(s32[1040]{0:T(1024)S(1)} %fusion.44, bf16[1040,256]{1,0:T(8,128)(2,1)S(1)} %scatter_custom_fusion.5, bf16[]{:T(256)} %constant.49.clone.1), kind=kCustom, calls=%fused_computation.21 | custom fusion | bytes 557058 | tf_op jit(solution)/shard_map/scatter | solution.py:55
  152.7 1.1 reshape.420
  153.8 17.2 %all-to-all-done = bf16[64,17,256]{2,1,0:T(8,128)(2,1)S(1)} async-done(((bf16[64,17,256]{2,1,0:T(8,128)(2,1)}), bf16[64,17,256]{2,1,0:T(8,128)(2,1)S(1)}, u32[]{:S(2)}, u32[]{:S(2)}) %all-to-all-start) | async-done | bytes 557088 | tf_op jit(solution)/shard_map/all_to_all | solution.py:59
  171.0 9.7 %all-to-all-start.1 = ((bf16[64,17,256]{2,1,0:T(8,128)(2,1)}), bf16[64,17,256]{2,1,0:T(8,128)(2,1)S(1)}, u32[]{:S(2)}, u32[]{:S(2)}) async-start(bf16[64,17,256]{2,1,0:T(8,128)(2,1)} %reshape.420), calls=%async_computation.1 | async-start | bytes 1572864 | tf_op jit(solution)/shard_map/all_to_all | solution.py:59
  180.8 0.2 lt.95
  181.0 0.1 add.229
  181.2 1.3 dynamic-slice.1
  183.1 0.1 fusion.24
  183.3 0.1 reduce.10
  183.4 0.1 reshape.511
  183.6 0.1 reduce.12
  183.7 0.2 reshape.543
  183.8 12.6 %scatter_custom_fusion.10 = bf16[1040]{0:T(1024)(128)(2,1)S(1)} fusion(s32[1088]{0:T(1024)S(1)} %fusion.43, bf16[1088]{0:T(1024)(128)(2,1)S(1)} %reshape.511, bf16[]{:T(256)} %constant.49.clone.1), kind=kCustom, calls=%fused_computation.103 | custom fusion | bytes 2082 | tf_op jit(solution)/shard_map/scatter | solution.py:79
  196.5 13.1 %scatter_custom_fusion.14 = bf16[1040]{0:T(1024)(128)(2,1)S(1)} fusion(s32[1088]{0:T(1024)S(1)} %fusion.43, bf16[1088]{0:T(1024)(128)(2,1)S(1)} %reshape.543, bf16[]{:T(256)} %constant.99.clone.1), kind=kCustom, calls=%fused_computation.97 | custom fusion | bytes 2082 | tf_op jit(solution)/shard_map/scatter | solution.py:79
  209.6 0.2 reshape.455
  209.8 7.9 %scatter_custom_fusion.3 = bf16[1040,256]{1,0:T(8,128)(2,1)S(1)} fusion(s32[1088]{0:T(1024)S(1)} %fusion.43, bf16[1088,256]{1,0:T(8,128)(2,1)S(1)} %reshape.455, bf16[]{:T(256)} %constant.49.clone.1), kind=kCustom, calls=%fused_computation.29 | custom fusion | bytes 532482 | tf_op jit(solution)/shard_map/scatter | solution.py:79
  217.8 0.2 reshape.487
  218.0 7.9 %scatter_custom_fusion.7 = bf16[1040,256]{1,0:T(8,128)(2,1)S(1)} fusion(s32[1088]{0:T(1024)S(1)} %fusion.43, bf16[1088,256]{1,0:T(8,128)(2,1)S(1)} %reshape.487, bf16[]{:T(256)} %constant.49.clone.1), kind=kCustom, calls=%fused_computation.25 | custom fusion | bytes 532482 | tf_op jit(solution)/shard_map/scatter | solution.py:79
  225.9 0.4 fusion.67
  226.3 0.2 fusion.16
  226.6 115.0 %pmax.7 = f32[1,48]{1,0:T(1,128)S(1)} all-reduce(f32[1,48]{1,0:T(1,128)S(1)} %bitcast.94), channel_id=1, replica_groups=mesh['seq'=64,'tp'=8] {'seq'}, use_global_device_ids=true, to_apply=%region_24.25 | all-reduce | flops 48 | bytes 384 | tf_op jit(solution)/shard_map/pmax | solution.py:161
  341.6 0.3 fusion.3
  341.9 219.7 %all-reduce.2 = (f32[1,48,256]{2,1,0:T(8,128)S(1)}, f32[1,48]{1,0:T(1,128)S(1)}) all-reduce(f32[1,48,256]{2,1,0:T(8,128)S(1)} %fusion.3, f32[1,48]{1,0:T(1,128)S(1)} %get-tuple-element.16), channel_id=1, replica_groups=mesh['seq'=64,'tp'=8] {'seq'}, use_global_device_ids=true, to_apply=%region_25.26 | all-reduce | flops 12336 | bytes 98688 | tf_op jit(solution)/shard_map/psum | solution.py:163
  561.6 0.2 fusion.25
  561.8 107.3 %all-reduce.1 = bf16[48,32]{1,0:T(8,128)(2,1)S(1)} all-reduce(f32[48,32]{1,0:T(8,128)S(1)} %fusion.25), channel_id=2, replica_groups=mesh['seq'=64,'tp'=8] {'tp'}, use_global_device_ids=true, to_apply=%region_28.29.clone | all-reduce | flops 1536 | bytes 9216
  669.1 0.6 dynamic-slice_convert_fusion
  (43 shorter events, 0.6 us)
Async XLA Ops:
  0.6 561.0 %copy-start = (bf16[256,32]{0,1:T(8,128)(2,1)S(1)}, bf16[256,32]{0,1:T(8,128)(2,1)}, u32[]{:S(2)}) copy-start(bf16[256,32]{0,1:T(8,128)(2,1)} %param.17) | copy-start | bytes 49156
  51.6 7.6 %copy-start.5 = (s32[2048]{0:T(1024)S(1)}, s32[2048]{0:T(1024)}, u32[]{:S(2)}) copy-start(s32[2048]{0:T(1024)} %param.11) | copy-start | bytes 24580
  51.6 33.6 %all-to-all-start.2 = ((bf16[64,1,17]{2,1,0:T(2,128)(2,1)}), bf16[64,1,17]{2,1,0:T(2,128)(2,1)S(1)}, u32[]{:S(2)}, u32[]{:S(2)}) async-start(bf16[64,1,17]{2,1,0:T(2,128)(2,1)} %all_to_all.24), calls=%async_computation.2 | async-start | bytes 65536 | tf_op jit(solution)/shard_map/all_to_all | solution.py:59
  59.5 0.7 copy-start.10
  60.3 0.7 copy-start.7
  85.1 34.4 %all-to-all-start.3 = ((bf16[64,1,17]{2,1,0:T(2,128)(2,1)}), bf16[64,1,17]{2,1,0:T(2,128)(2,1)S(1)}, u32[]{:S(2)}, u32[]{:S(2)}) async-start(bf16[64,1,17]{2,1,0:T(2,128)(2,1)} %all_to_all.25), calls=%async_computation.3 | async-start | bytes 65536 | tf_op jit(solution)/shard_map/all_to_all | solution.py:59
  119.5 14.7 %copy-start.3 = (bf16[2048,256]{1,0:T(8,128)(2,1)S(1)}, bf16[2048,256]{1,0:T(8,128)(2,1)}, u32[]{:S(2)}) copy-start(bf16[2048,256]{1,0:T(8,128)(2,1)} %param.10) | copy-start | bytes 3145732
  119.5 51.5 %all-to-all-start = ((bf16[64,17,256]{2,1,0:T(8,128)(2,1)}), bf16[64,17,256]{2,1,0:T(8,128)(2,1)S(1)}, u32[]{:S(2)}, u32[]{:S(2)}) async-start(bf16[64,17,256]{2,1,0:T(8,128)(2,1)} %reshape.417), calls=%async_computation | async-start | bytes 1572864 | tf_op jit(solution)/shard_map/all_to_all | solution.py:59
  171.0 46.8 %all-to-all-start.1 = ((bf16[64,17,256]{2,1,0:T(8,128)(2,1)}), bf16[64,17,256]{2,1,0:T(8,128)(2,1)S(1)}, u32[]{:S(2)}, u32[]{:S(2)}) async-start(bf16[64,17,256]{2,1,0:T(8,128)(2,1)} %reshape.420), calls=%async_computation.1 | async-start | bytes 1572864 | tf_op jit(solution)/shard_map/all_to_all | solution.py:59
  181.0 2.1 copy-start.6
  181.0 2.1 copy-start.8
  196.5 13.1 %copy-start.9 = (bf16[1040]{0:T(1024)(128)(2,1)}, bf16[1040]{0:T(1024)(128)(2,1)S(1)}, u32[]{:S(2)}) copy-start(bf16[1040]{0:T(1024)(128)(2,1)S(1)} %scatter_custom_fusion.10) | copy-start | bytes 6244
  209.6 132.0 %copy-start.4 = (s32[1040]{0:T(1024)}, s32[1040]{0:T(1024)S(1)}, u32[]{:S(2)}) copy-start(s32[1040]{0:T(1024)S(1)} %convert_element_type.63) | copy-start | bytes 12484
  217.8 8.2 %copy-start.1 = (bf16[1040,256]{1,0:T(8,128)(2,1)}, bf16[1040,256]{1,0:T(8,128)(2,1)S(1)}, u32[]{:S(2)}) copy-start(bf16[1040,256]{1,0:T(8,128)(2,1)S(1)} %scatter_custom_fusion.3) | copy-start | bytes 1597444
  225.9 115.9 %copy-start.2 = (bf16[1040,256]{1,0:T(8,128)(2,1)}, bf16[1040,256]{1,0:T(8,128)(2,1)S(1)}, u32[]{:S(2)}) copy-start(bf16[1040,256]{1,0:T(8,128)(2,1)S(1)} %scatter_custom_fusion.7) | copy-start | bytes 1597444
  341.9 219.7 %copy-start.11 = (bf16[48,256]{1,0:T(8,128)(2,1)S(1)}, bf16[48,256]{1,0:T(8,128)(2,1)}, u32[]{:S(2)}) copy-start(bf16[48,256]{1,0:T(8,128)(2,1)} %param.16) | copy-start | bytes 73732
where the time goes:
time: 677 us; the launch traced here: 670 us
  blocking collectives  472 us (70%)
  local copies, waits for them, and re-layouts  123 us (18%)
  starting transfers between devices  46.4 us (7%)
  waiting for transfers between devices  17.2 us (3%)
  other arithmetic  6.82 us (1%)
    psum x1, blocking collectives, on_device(): lax.psum((softmax_parts[1] * rescale, softmax_parts[2] * rescale[:, :, No...  220 us
    unnamed x2, blocking collectives  137 us
    pmax x1, blocking collectives, on_device(): peak_score = lax.pmax(softmax_parts[0], 'seq')  115 us
    all_to_all x4, starting transfers between devices, repack(): lax.all_to_all(shortened(tuple((pack_peers(item) for item in entries))),...  46.4 us
    scatter x4, local copies, waits for them, and re-layouts, unpack_peers(): return jnp.full((slot_count,) + array.shape[2:], fill_value, array.dtype)...  41.6 us
    scatter x4, local copies, waits for them, and re-layouts, pack_peers(): buffer = jnp.zeros((seq_count * peer_slots,) + array.shape[1:], array.dty...  41.1 us
    all_to_all x4, waiting for transfers between devices, repack(): lax.all_to_all(shortened(tuple((pack_peers(item) for item in entries))),...  17.2 us
  transfers between devices with their start and end apart: 4, of which 1 were waited for; matrix products, arithmetic and copies ran while one was open for 15% of the time, Pallas kernels for 0%

commit v1 on v0

v1 whole, which is shorter than its diff:
```python
import jax
import jax.numpy as jnp
from jax import lax
from jax.experimental import pallas as pl
from jax.experimental.pallas import tpu as pltpu
from jax.sharding import PartitionSpec as P

MESH = pl.DeviceIdType.MESH
F32, BF16, I32 = jnp.float32, jnp.bfloat16, jnp.int32

N = 64
TP = 8
HD = 256
BLOCK = 128
NB = 16
ROWS = 2048
REQS = 48
K_DEV = 1040
SLAB = 16
MAIN = N * SLAB
TILE = 208
TILES = K_DEV // TILE
NEG = -1e30


def iota(shape, dim):
    return lax.broadcasted_iota(I32, shape, dim)


def entry_of(t):
    return jnp.where(t < MAIN, (t & (SLAB - 1)) * N + (t >> 4), t)


def pack_kernel(
    k_ref, v_ref, keep_ref, w_ref, req_ref, q_ref, grp, counts, rsend, part
):
    me = lax.axis_index("seq")
    keep = keep_ref[...]
    keepf = keep.astype(F32)
    upper = (iota((BLOCK, BLOCK), 0) < iota((BLOCK, BLOCK), 1)).astype(BF16)
    within = jnp.dot(keepf.astype(BF16), upper, preferred_element_type=F32)
    kept_col = jnp.sum(keepf, axis=1, keepdims=True)
    size_col = kept_col + 1.0
    eye = iota((NB, BLOCK), 0) == iota((NB, BLOCK), 1)
    size_row = jnp.sum(jnp.where(eye, size_col, 0.0), axis=0, keepdims=True)
    base_col = jnp.sum(
        jnp.where(iota((NB, BLOCK), 1) < iota((NB, BLOCK), 0), size_row, 0.0), axis=1, keepdims=True
    )
    fold_col = base_col + kept_col
    counts[...] = size_row.astype(I32)
    entry = jnp.where(keep == 1, base_col + within, fold_col).astype(I32)
    tgt_in = jnp.where(entry < MAIN, ((entry & (N - 1)) << 4) | (entry >> 6), entry)
    dropped = w_ref[...] * (1 - keep)
    val_in = jnp.where(keep == 1, 1, dropped).astype(F32)
    denom_col = jnp.sum(dropped.astype(F32), axis=1, keepdims=True)
    inv_row = jnp.sum(jnp.where(eye, 1.0 / denom_col, 0.0), axis=0, keepdims=True)
    fold_row = jnp.sum(jnp.where(eye, fold_col, 0.0), axis=0, keepdims=True).astype(I32)
    fold_row = jnp.where(iota((1, BLOCK), 1) < NB, fold_row, -1)

    def group(j, _):
        start = pl.multiple_of(j * TILE, 16)
        t = iota((TILE, BLOCK), 0) + start
        pieces = [
            jnp.where(t == tgt_in[b : b + 1, :], val_in[b : b + 1, :], 0.0).astype(BF16)
            for b in range(NB)
        ]
        sel = jnp.concatenate(pieces, axis=1)
        is_fold = entry_of(t) == fold_row
        scale = jnp.sum(jnp.where(is_fold, inv_row, 0.0), axis=1, keepdims=True)
        scale = jnp.where(scale > 0.0, scale, 1.0)
        kk = jnp.dot(sel, k_ref[...], preferred_element_type=F32)
        vv = jnp.dot(sel, v_ref[...], preferred_element_type=F32)
        grp[pl.ds(start, TILE), 0:HD] = (kk * scale).astype(BF16)
        grp[pl.ds(start, TILE), HD : 2 * HD] = (vv * scale).astype(BF16)
        return 0

    lax.fori_loop(0, TILES, group, 0)

    spread = spread_rows()
    q64 = jnp.dot(spread, q_ref[...], preferred_element_type=F32)
    srow = iota((N, BLOCK), 0)
    lane = iota((N, BLOCK), 1)
    used = (srow & 7) < 6
    starts, ends = request_blocks(req_ref)
    gblock = (lane + me * NB).astype(F32)
    low = jnp.sum(jnp.where(gblock < starts, size_row, 0.0), axis=1, keepdims=True)
    high = jnp.sum(jnp.where((gblock < ends) & used, size_row, 0.0), axis=1, keepdims=True)
    log_col = jnp.log(float(BLOCK) - kept_col).astype(BF16).astype(F32)
    e_row = entry_of(iota((1, K_DEV), 1)).astype(F32)
    bias_row = jnp.sum(
        jnp.where(jnp.broadcast_to(e_row, (NB, K_DEV)) == fold_col, log_col, 0.0), axis=0, keepdims=True
    )
    scores = lax.dot_general(
        q64.astype(BF16), grp[:, 0:HD], (((1,), (1,)), ((), ())), preferred_element_type=F32
    )
    scores = scores * (1.0 / 16.0) + bias_row
    member = (e_row >= low) & (e_row < high)
    scores = jnp.where(member, scores, NEG)
    peak = jnp.max(scores, axis=1, keepdims=True)
    probs = jnp.where(member, jnp.exp(scores - peak), 0.0)
    total = jnp.sum(probs, axis=1, keepdims=True)
    part[:, 0:HD] = jnp.dot(probs.astype(BF16), grp[:, HD : 2 * HD], preferred_element_type=F32)
    part[:, HD : HD + 128] = jnp.broadcast_to(peak, (N, 128))
    part[:, HD + 128 : HD + 256] = jnp.broadcast_to(total, (N, 128))

    def fill_part(s, _):
        rsend[s] = part[pl.ds(s, 1), :]
        return 0

    lax.fori_loop(0, N, fill_part, 0)


def spread_rows():
    row, req = iota((N, REQS), 0), iota((N, REQS), 1)
    return ((6 * (row >> 3) + (row & 7) == req) & ((row & 7) < 6)).astype(BF16)


def request_blocks(req_ref):
    srow = iota((N, BLOCK), 0)
    lane = iota((N, BLOCK), 1)
    rid = 6 * (srow >> 3) + (srow & 7)
    req_row = req_ref[...].astype(F32)
    ends = jnp.sum(jnp.where(lane <= rid, req_row, 0.0), axis=1, keepdims=True)
    starts = jnp.sum(jnp.where(lane < rid, req_row, 0.0), axis=1, keepdims=True)
    return starts, ends


def turn_kernel(counts, grp, rrecv, q_ref, nk_ref, nv_ref, send, xsend, gsend, xf):
    me = lax.axis_index("seq")

    def sum_before(s, carry):
        return carry + jnp.where(s < me, counts[s], 0)

    before = lax.fori_loop(0, N, sum_before, jnp.zeros((1, BLOCK), I32))
    offset = jnp.sum(before)
    xf[...] = grp[MAIN:K_DEV, :].astype(F32)

    def turn(p, _):
        c = (p - offset) & (N - 1)
        send[p] = grp[pl.ds(pl.multiple_of(c * SLAB, SLAB), SLAB), :]
        row = xf[pl.ds(c & 15, 1), :]
        xsend[p] = jnp.concatenate([row[:, 0:HD], row[:, HD : 2 * HD]], axis=0).astype(BF16)
        return 0

    lax.fori_loop(0, N, turn, 0)

    mine = ((6 * (me >> 3) + (me & 7) == iota((8, REQS), 1)) & ((me & 7) < 6)).astype(BF16)
    qr = jnp.dot(mine, q_ref[...], preferred_element_type=F32)
    kr = jnp.dot(mine, nk_ref[...], preferred_element_type=F32)
    nv = jnp.dot(mine, nv_ref[...], preferred_element_type=F32)[0:1, :]
    own = jnp.sum(qr * kr, axis=1, keepdims=True)[0:1, :] * (1.0 / 16.0)
    own = jnp.broadcast_to(own, (1, 128))

    def top(i, carry):
        return jnp.maximum(carry, rrecv[i][:, HD : HD + 128])

    peak = lax.fori_loop(0, N, top, own)

    def merge(i, carry):
        tot, wsum = carry
        row = rrecv[i]
        w = jnp.exp(row[:, HD : HD + 128] - peak)
        tot = tot + w * row[:, HD + 128 : HD + 256]
        wsum = wsum + jnp.concatenate([w, w], axis=1) * row[:, 0:HD]
        return tot, wsum

    own_p = jnp.exp(own - peak)
    first = (own_p, jnp.concatenate([own_p, own_p], axis=1) * nv)
    tot, wsum = lax.fori_loop(0, N, merge, first, unroll=8)
    gsend[...] = (wsum / jnp.concatenate([tot, tot], axis=1)).astype(BF16).astype(F32)


def project_kernel(grecv, ow_ref, tsend, a2):
    def fill_rows(s, _):
        a2[pl.ds(s, 1), :] = grecv[s]
        return 0

    lax.fori_loop(0, N, fill_rows, 0)
    wide = jnp.dot(a2[...].astype(BF16), ow_ref[...], preferred_element_type=F32)
    for p in range(TP):
        tsend[p] = wide[8 * p : 8 * p + 8, :]


def place_kernel(counts, recv, xrecv, req_ref, pk_ref, pv_ref, pb_ref, pr_ref, c2, x2, tgt):
    me = lax.axis_index("seq")
    srow = iota((N, BLOCK), 0)
    lane = iota((N, BLOCK), 1)
    _, ends = request_blocks(req_ref)

    def fill_counts(s, _):
        c2[pl.ds(s, 1), :] = counts[s]
        return 0

    lax.fori_loop(0, N, fill_counts, 0)
    sizes = c2[...].astype(F32)
    sizes16 = sizes.astype(BF16)
    n_col = jnp.sum(sizes, axis=1, keepdims=True)
    before64 = (iota((N, N), 1) < iota((N, N), 0)).astype(BF16)
    off_col = jnp.sum(jnp.dot(before64, sizes16, preferred_element_type=F32), axis=1, keepdims=True)
    upto = (iota((BLOCK, BLOCK), 0) <= iota((BLOCK, BLOCK), 1)).astype(BF16)
    block_end = off_col + jnp.dot(sizes16, upto, preferred_element_type=F32)
    drops = jnp.where(lane < NB, float(BLOCK + 1) - sizes, 1.0)
    logs = jnp.log(drops).astype(BF16).astype(F32)
    j_row = (iota((1, K_DEV), 1) * N + me).astype(F32)
    bias_out = jnp.zeros((N, K_DEV), F32)
    for b in range(NB):
        hit = (block_end[:, b : b + 1] - 1.0) == j_row
        bias_out = jnp.where(hit, logs[:, b : b + 1], bias_out)
    pb_ref[...] = jnp.sum(bias_out, axis=0, keepdims=True).astype(BF16)
    last = ends.astype(I32) - 1
    pick = (iota((N, N), 1) == (last >> 4)).astype(F32)
    picked = jnp.dot(pick, block_end, preferred_element_type=F32, precision=lax.Precision.HIGHEST)
    req_end = jnp.sum(jnp.where(lane == (last & 15), picked, 0.0), axis=1, keepdims=True)
    past = ((req_end <= j_row) & ((iota((N, K_DEV), 0) & 7) < 6)).astype(F32)
    owner = jnp.sum(past, axis=0, keepdims=True)
    every = jnp.sum(n_col, axis=0, keepdims=True)
    pr_ref[...] = jnp.where(j_row < every, owner, -1.0).astype(I32)

    off_i = off_col.astype(I32)
    c_col = (me - off_i) & (N - 1)
    k0_col = ((off_i + c_col) >> 6).astype(F32)
    lim_col = n_col - c_col.astype(F32)
    col = iota((N, MAIN), 1)
    is_src = iota((N, MAIN), 0) == (col >> 4)
    k0 = jnp.sum(jnp.where(is_src, k0_col, 0.0), axis=0, keepdims=True)
    lim = jnp.sum(jnp.where(is_src, lim_col, 0.0), axis=0, keepdims=True)
    q = (col[0:1, :] & (SLAB - 1)).astype(F32)
    tgt[...] = jnp.where(q * N < lim, k0 + q, -1.0).astype(I32)
    is_src = srow == lane
    k0 = jnp.sum(jnp.where(is_src, k0_col, 0.0), axis=0, keepdims=True)
    lim = jnp.sum(jnp.where(is_src, lim_col, 0.0), axis=0, keepdims=True)
    xtgt = jnp.where(lim > float(MAIN), k0 + float(SLAB), -1.0).astype(I32)
    x2[...] = jnp.zeros(x2.shape, F32)

    def fill_extra(i, _):
        pair = xrecv[i].astype(F32)
        x2[pl.ds(i, 1), 0:HD] = pair[0:1, :]
        x2[pl.ds(i, 1), HD : 2 * HD] = pair[1:2, :]
        return 0

    lax.fori_loop(0, N, fill_extra, 0)

    def place(j, _):
        start = pl.multiple_of(j * TILE, 16)
        sel = jnp.where(iota((TILE, MAIN), 0) + start == tgt[...], 1.0, 0.0).astype(BF16)
        xsel = jnp.where(iota((TILE, BLOCK), 0) + start == xtgt, 1.0, 0.0).astype(BF16)
        rows = recv[...].reshape(MAIN, 2 * HD)
        got = jnp.dot(sel, rows, preferred_element_type=F32)
        got = got + jnp.dot(xsel, x2[...].astype(BF16), preferred_element_type=F32)
        pk_ref[pl.ds(start, TILE), :] = got[:, 0:HD].astype(BF16)
        pv_ref[pl.ds(start, TILE), :] = got[:, HD : 2 * HD].astype(BF16)
        return 0

    lax.fori_loop(0, TILES, place, 0)


def exchange_counts(counts, rsend):
    counts = lax.all_gather(counts, "seq", axis=0, tiled=False)
    return counts, lax.all_to_all(rsend, "seq", split_axis=0, concat_axis=0, tiled=True)


def exchange_main(send, xsend, gsend):
    recv = lax.all_to_all(send, "seq", split_axis=0, concat_axis=0, tiled=True)
    xrecv = lax.all_to_all(xsend, "seq", split_axis=0, concat_axis=0, tiled=True)
    return recv, xrecv, lax.all_gather(gsend, "seq", axis=0, tiled=False)


def exchange_tp(tsend):
    mine = lax.psum_scatter(tsend, "tp", scatter_dimension=0, tiled=False)
    return mine[0:6, 0:32].astype(BF16)


def local(body, name, outs, scratch, *args):
    vmem = pl.BlockSpec(memory_space=pltpu.VMEM)
    return pl.pallas_call(
        body,
        name=name,
        out_shape=tuple(jax.ShapeDtypeStruct(s, d) for s, d in outs),
        in_specs=[vmem] * len(args),
        out_specs=(vmem,) * len(outs),
        scratch_shapes=[pltpu.VMEM(s, d) for s, d in scratch],
        compiler_params=pltpu.CompilerParams(vmem_limit_bytes=40 << 20),
    )(*args)


def on_device(ck, cv, keep, w, req, q, nk, nv, ow):
    keep2 = keep.reshape(NB, BLOCK)
    w2 = w.reshape(NB, BLOCK)
    req2 = jnp.pad(req, (0, BLOCK - REQS)).reshape(1, BLOCK)
    ow2 = jnp.pad(ow, ((0, 0), (0, 128 - ow.shape[1])))
    grp, counts, rsend = local(
        pack_kernel, "pack",
        [((K_DEV, 2 * HD), BF16), ((1, BLOCK), I32), ((N, 1, 2 * HD), F32)],
        [((N, 2 * HD), F32)],
        ck, cv, keep2, w2, req2, q,
    )
    counts, rrecv = exchange_counts(counts, rsend)
    send, xsend, gsend = local(
        turn_kernel, "turn",
        [((N, SLAB, 2 * HD), BF16), ((N, 2, HD), BF16), ((1, HD), F32)],
        [((16, 2 * HD), F32)],
        counts, grp, rrecv, q, nk, nv,
    )
    recv, xrecv, grecv = exchange_main(send, xsend, gsend)
    (tsend,) = local(project_kernel, "project", [((TP, 8, 128), F32)], [((N, HD), F32)], grecv, ow2)
    lo = exchange_tp(tsend)
    pk, pv, pb, pr = local(
        place_kernel, "place",
        [((K_DEV, HD), BF16), ((K_DEV, HD), BF16), ((1, K_DEV), BF16), ((1, K_DEV), I32)],
        [((N, BLOCK), I32), ((BLOCK, 2 * HD), F32), ((1, MAIN), I32)],
        counts, recv, xrecv, req2,
    )
    return pk, pv, pb.reshape(K_DEV), pr.reshape(K_DEV), lo


def solution(mesh):
    in_specs = (
        P("seq", "tp"), P("seq", "tp"), P("seq"), P("seq"), P(),
        P(None, "tp"), P(None, "tp"), P(None, "tp"), P("tp", "seq"),
    )
    out_specs = (P("seq", "tp"), P("seq", "tp"), P("seq"), P("seq"), P("tp", "seq"))
    return jax.shard_map(on_device, mesh=mesh, in_specs=in_specs, out_specs=out_specs, check_vma=False)
```

time: 677 us -> 274 us (0.40)
  blocking collectives: 472 us -> 225 us
  local copies, waits for them, and re-layouts: 123 us -> 7.88 us
  starting transfers between devices: 46.4 us -> 23.9 us
  waiting for transfers between devices: 17.2 us -> 0.01 us
  Pallas kernels: 0 us -> 13.4 us
    psum x1 -> x0, blocking collectives: 220 us -> none  [on_device(): lax.psum((softmax_parts[1] * rescale, softmax_parts[2] * rescale[:, :, No...]
    all_gather x0 -> x2, blocking collectives: none -> 152 us  [the longest x1 90.9 us: exchange_main(): return (recv, xrecv, lax.all_gather(gsend, 'seq', axis=0, tiled=False))]
    pmax x1 -> x0, blocking collectives: 115 us -> none  [on_device(): peak_score = lax.pmax(softmax_parts[0], 'seq')]
    scatter x13 -> x0, local copies, waits for them, and re-layouts: 111 us -> none  [the longest x4 41.6 us: unpack_peers(): return jnp.full((slot_count,) + array.shape[2:], fill_value, array.dtype)...]
    unnamed x2 -> x1, blocking collectives: 137 us -> 51.1 us
    all_to_all x4 -> x2, starting transfers between devices: 46.4 us -> 23.9 us  [the longest x1 19.1 us: exchange_counts(): lax.all_to_all(rsend, 'seq', split_axis=0, concat_axis=0, tiled=True)]
    all_to_all x0 -> x1, blocking collectives: none -> 22.1 us  [exchange_main(): lax.all_to_all(xsend, 'seq', split_axis=0, concat_axis=0, tiled=True)]
    all_to_all x4 -> x2, waiting for transfers between devices: 17.2 us -> 0.01 us  [the longest x1 0.01 us: exchange_main(): recv = lax.all_to_all(send, 'seq', split_axis=0, concat_axis=0, tiled=True)]
  transfers between devices with their start and end apart: 4 -> 2, of which waited for: 1 -> 0; matrix products, arithmetic and copies ran while one was open for 15% -> 1% of each run, Pallas kernels for 0% -> 0%
where the time goes in v1:
time: 274 us; the launch traced here: 272 us
  blocking collectives  225 us (82%)
  starting transfers between devices  23.9 us (9%)
  Pallas kernels  13.4 us (5%)
  local copies, waits for them, and re-layouts  7.88 us (3%)
    all_gather x1, blocking collectives, exchange_main(): return (recv, xrecv, lax.all_gather(gsend, 'seq', axis=0, tiled=False))  90.9 us
    all_gather x1, blocking collectives, exchange_counts(): counts = lax.all_gather(counts, 'seq', axis=0, tiled=False)  60.9 us
    unnamed x1, blocking collectives  51.1 us
    all_to_all x1, blocking collectives, exchange_main(): lax.all_to_all(xsend, 'seq', split_axis=0, concat_axis=0, tiled=True)  22.1 us
    all_to_all x1, starting transfers between devices, exchange_counts(): lax.all_to_all(rsend, 'seq', split_axis=0, concat_axis=0, tiled=True)  19.1 us
    pallas_call x4, Pallas kernels, local(): pl.pallas_call(body, name=name, out_shape=tuple((jax.ShapeDtypeStruct(s,...  13.4 us
    unnamed x20, local copies, waits for them, and re-layouts  5.98 us
  transfers between devices with their start and end apart: 2, of which 0 were waited for; matrix products, arithmetic and copies ran while one was open for 1% of the time, Pallas kernels for 0%

profile of v1, /device:TPU:1, one launch (start us, length us, event | category | flops | bytes accessed | tf_op | source)
XLA Modules:
  0.0 272.1 jit_solution(1586050280993252144)
XLA Ops:
  0.6 0.7 pad_bitcast_fusion.req_ref
  1.3 0.0 copy-start
  1.3 1.2 copy-done
  2.5 0.0 copy-start.1
  2.5 1.2 copy-done.1
  3.7 0.0 copy-start.2
  3.7 0.7 copy-done.2
  4.5 0.0 copy-start.6
  4.5 0.7 copy-done.6
  5.2 0.0 copy-start.7
  5.2 0.7 copy-done.7
  5.9 0.0 copy-start.3
  5.9 0.0 copy-start.4
  5.9 0.0 copy-start.5
  5.9 5.1 %pack.1 = (bf16[1040,512]{1,0:T(8,128)(2,1)S(1)}, s32[1,128]{1,0:T(1,128)S(1)}, f32[64,1,512]{2,1,0:T(1,128)}) custom-call(bf16[2048,256]{1,0:T(8,128)(2,1)S(1)} %copy-done, bf16[2048,256]{1,0:T(8,128)(2,1)S(1)} %copy-done.1, s32[16,128]{1,0:T(8,128)S(1)} %bitcast.10, s32[16,128]{1,0:T(8,128)S(1)} %bitcast.11, s32[1,128]{1,0:T(1,128)S(1)} %pad_bitcast_fusion.req_ref, ...), custom_call_target="tpu_custom_call" | custom-call | tf_op jit(solution)/shard_map/pack/pallas_call | solution.py:275
  11.0 19.1 %all-to-all-start = ((f32[64,1,512]{2,1,0:T(1,128)}), f32[64,1,512]{2,1,0:T(1,128)S(1)}, u32[]{:S(2)}, u32[]{:S(2)}) async-start(f32[64,1,512]{2,1,0:T(1,128)} %get-tuple-element.17), calls=%async_computation | async-start | bytes 262144 | tf_op jit(solution)/shard_map/all_to_all | solution.py:259
  30.1 60.9 %all-gather.2.counts = s32[64,1,128]{2,1,0:T(1,128)S(1)} all-gather(s32[1,1,128]{2,1,0:T(1,128)S(1)} %bitcast.13), channel_id=2, replica_groups=mesh['seq'=64,'tp'=8] {'seq'}, dimensions={0}, use_global_device_ids=true | all-gather | bytes 33280 | tf_op jit(solution)/shard_map/all_gather | solution.py:258
  91.0 0.0 all-to-all-done.rrecv
  91.0 0.0 copy-done.3
  91.0 0.0 copy-done.4
  91.0 0.0 copy-done.5
  91.0 2.9 %turn.1 = (bf16[64,16,512]{2,1,0:T(8,128)(2,1)}, bf16[64,2,256]{2,1,0:T(2,128)(2,1)S(1)}, f32[1,256]{1,0:T(1,128)S(1)}) custom-call(s32[64,1,128]{2,1,0:T(1,128)S(1)} %all-gather.2.counts, bf16[1040,512]{1,0:T(8,128)(2,1)S(1)} %get-tuple-element.16.grp, f32[64,1,512]{2,1,0:T(1,128)S(1)} %all-to-all-done.rrecv, bf16[48,256]{1,0:T(8,128)(2,1)S(1)} %copy-done.3, ...), custom_call_target="tpu_custom_call" | custom-call | tf_op jit(solution)/shard_map/turn/pallas_call | solution.py:275
  93.9 22.1 %all_to_all.15.xrecv = bf16[64,2,256]{2,1,0:T(2,128)(2,1)S(1)} all-to-all(bf16[64,2,256]{2,1,0:T(2,128)(2,1)S(1)} %get-tuple-element.19), channel_id=1, replica_groups=mesh['seq'=64,'tp'=8] {'seq'}, dimensions={0} | all-to-all | bytes 131072 | tf_op jit(solution)/shard_map/all_to_all | solution.py:264
  116.0 0.0 copy-start.8
  116.0 4.8 %all-to-all-start.1 = ((bf16[64,16,512]{2,1,0:T(8,128)(2,1)}), bf16[64,16,512]{2,1,0:T(8,128)(2,1)S(1)}, u32[]{:S(2)}, u32[]{:S(2)}) async-start(bf16[64,16,512]{2,1,0:T(8,128)(2,1)} %get-tuple-element.18), calls=%async_computation.1 | async-start | bytes 2097152 | tf_op jit(solution)/shard_map/all_to_all | solution.py:263
  120.8 0.0 copy-done.8
  120.8 0.1 copy.15
  121.0 1.3 dynamic-slice
  122.2 90.9 %all-gather.3.grecv = f32[64,1,256]{2,1,0:T(1,128)S(1)} all-gather(f32[1,1,256]{2,1,0:T(1,128)S(1)} %bitcast.12), channel_id=3, replica_groups=mesh['seq'=64,'tp'=8] {'seq'}, dimensions={0}, use_global_device_ids=true | all-gather | bytes 66560 | tf_op jit(solution)/shard_map/all_gather | solution.py:265
  213.1 0.5 project.1
  213.6 51.1 %all-reduce.2 = bf16[8,8,128]{2,1,0:T(8,128)(2,1)S(1)} all-reduce(f32[8,8,128]{2,1,0:T(8,128)S(1)} %project.1), channel_id=4, replica_groups=mesh['seq'=64,'tp'=8] {'tp'}, use_global_device_ids=true, to_apply=%region_0.1.clone | all-reduce | flops 8192 | bytes 49152
  264.7 1.2 fusion
  265.9 0.0 all-to-all-done.1.recv
  265.9 4.9 %place.1 = (bf16[1040,256]{1,0:T(8,128)(2,1)}, bf16[1040,256]{1,0:T(8,128)(2,1)}, bf16[1,1040]{1,0:T(2,128)(2,1)S(1)}, s32[1,1040]{1,0:T(1,128)S(1)}) custom-call(s32[64,1,128]{2,1,0:T(1,128)S(1)} %all-gather.2.counts, bf16[64,16,512]{2,1,0:T(8,128)(2,1)S(1)} %all-to-all-done.1.recv, bf16[64,2,256]{2,1,0:T(2,128)(2,1)S(1)} %all_to_all.15.xrecv, ...), custom_call_target="tpu_custom_call" | custom-call | tf_op jit(solution)/shard_map/place/pallas_call | solution.py:275
  270.8 0.6 reduce.1
  271.4 0.6 reduce
  (1 shorter events, 0.0 us)
Async XLA Ops:
  1.3 1.2 copy-start
  2.5 1.2 copy-start.1
  3.7 0.7 copy-start.2
  4.5 0.7 copy-start.6
  5.2 0.7 copy-start.7
  5.9 85.1 %copy-start.3 = (bf16[48,256]{1,0:T(8,128)(2,1)S(1)}, bf16[48,256]{1,0:T(8,128)(2,1)}, u32[]{:S(2)}) copy-start(bf16[48,256]{1,0:T(8,128)(2,1)} %q_ref.3) | copy-start | bytes 73732
  5.9 85.1 %copy-start.4 = (bf16[48,256]{1,0:T(8,128)(2,1)S(1)}, bf16[48,256]{1,0:T(8,128)(2,1)}, u32[]{:S(2)}) copy-start(bf16[48,256]{1,0:T(8,128)(2,1)} %nk_ref.1) | copy-start | bytes 73732
  5.9 85.1 %copy-start.5 = (bf16[48,256]{1,0:T(8,128)(2,1)S(1)}, bf16[48,256]{1,0:T(8,128)(2,1)}, u32[]{:S(2)}) copy-start(bf16[48,256]{1,0:T(8,128)(2,1)} %nv_ref.1) | copy-start | bytes 73732
  11.0 80.0 %all-to-all-start = ((f32[64,1,512]{2,1,0:T(1,128)}), f32[64,1,512]{2,1,0:T(1,128)S(1)}, u32[]{:S(2)}, u32[]{:S(2)}) async-start(f32[64,1,512]{2,1,0:T(1,128)} %get-tuple-element.17), calls=%async_computation | async-start | bytes 262144 | tf_op jit(solution)/shard_map/all_to_all | solution.py:259
  116.0 4.8 %copy-start.8 = (bf16[256,32]{0,1:T(8,128)(2,1)S(1)}, bf16[256,32]{0,1:T(8,128)(2,1)}, u32[]{:S(2)}) copy-start(bf16[256,32]{0,1:T(8,128)(2,1)} %param.17) | copy-start | bytes 49156
  116.0 149.9 %all-to-all-start.1 = ((bf16[64,16,512]{2,1,0:T(8,128)(2,1)}), bf16[64,16,512]{2,1,0:T(8,128)(2,1)S(1)}, u32[]{:S(2)}, u32[]{:S(2)}) async-start(bf16[64,16,512]{2,1,0:T(8,128)(2,1)} %get-tuple-element.18), calls=%async_computation.1 | async-start | bytes 2097152 | tf_op jit(solution)/shard_map/all_to_all | solution.py:263

commit v2 on v1

--- a/solution.py
+++ b/solution.py
@@ -254,20 +254,90 @@
     lax.fori_loop(0, TILES, place, 0)
 
 
+def remote(body, name, cid, outs, *args):
+    vmem = pl.BlockSpec(memory_space=pltpu.VMEM)
+    return pl.pallas_call(
+        body,
+        name=name,
+        out_shape=tuple(jax.ShapeDtypeStruct(s, d) for s, d in outs),
+        in_specs=[vmem] * len(args),
+        out_specs=(vmem,) * len(outs),
+        scratch_shapes=[pltpu.SemaphoreType.DMA] * (2 * len(outs) + 1),
+        compiler_params=pltpu.CompilerParams(
+            collective_id=cid, has_side_effects=True, vmem_limit_bytes=40 << 20
+        ),
+    )(*args)
+
+
+def swap(axis, count, moves, local_sem):
+    me = lax.axis_index(axis)
+
+    barrier = pltpu.get_barrier_semaphore()
+
+    def greet(i, _):
+        p = lax.rem(me + 1 + i, count)
+        pl.semaphore_signal(barrier, inc=1, device_id={axis: p}, device_id_type=MESH)
+        return 0
+
+    lax.fori_loop(0, count - 1, greet, 0)
+    for src, dst, whole, _, _ in moves:
+        copy = pltpu.make_async_copy(src if whole else src.at[me], dst.at[me], local_sem)
+        copy.start()
+        copy.wait()
+    pl.semaphore_wait(barrier, count - 1)
+
+    def go(i, _):
+        p = lax.rem(me + 1 + i, count)
+        for src, dst, whole, s_sem, r_sem in moves:
+            pltpu.make_async_remote_copy(
+                src if whole else src.at[p], dst.at[me], s_sem, r_sem,
+                device_id={axis: p}, device_id_type=MESH,
+            ).start()
+        return 0
+
+    lax.fori_loop(0, count - 1, go, 0)
+    for _, dst, _, s_sem, r_sem in moves:
+        many = dst.at[pl.ds(0, count - 1)]
+        wait = pltpu.make_async_remote_copy(
+            many, many, s_sem, r_sem, device_id={axis: lax.rem(me + 1, count)}, device_id_type=MESH
+        )
+        wait.wait_recv()
+        wait.wait_send()
+
+
+def counts_kernel(counts, rsend, call, rrecv, s0, r0, s1, r1, sem):
+    swap("seq", N, [(counts, call, True, s0, r0), (rsend, rrecv, False, s1, r1)], sem)
+
+
+def main_kernel(send, xsend, gsend, recv, xrecv, grecv, s0, r0, s1, r1, s2, r2, sem):
+    swap(
+        "seq", N,
+        [(gsend, grecv, True, s2, r2), (send, recv, False, s0, r0), (xsend, xrecv, False, s1, r1)],
+        sem,
+    )
+
+
+def tp_kernel(tsend, trecv, s0, r0, sem):
+    swap("tp", TP, [(tsend, trecv, False, s0, r0)], sem)
+
+
 def exchange_counts(counts, rsend):
-    counts = lax.all_gather(counts, "seq", axis=0, tiled=False)
-    return counts, lax.all_to_all(rsend, "seq", split_axis=0, concat_axis=0, tiled=True)
+    return remote(
+        counts_kernel, "swap_counts", 0, [((N, 1, BLOCK), I32), ((N, 1, 2 * HD), F32)], counts, rsend
+    )
 
 
 def exchange_main(send, xsend, gsend):
-    recv = lax.all_to_all(send, "seq", split_axis=0, concat_axis=0, tiled=True)
-    xrecv = lax.all_to_all(xsend, "seq", split_axis=0, concat_axis=0, tiled=True)
-    return recv, xrecv, lax.all_gather(gsend, "seq", axis=0, tiled=False)
+    return remote(
+        main_kernel, "swap_main", 1,
+        [((N, SLAB, 2 * HD), BF16), ((N, 2, HD), BF16), ((N, 1, HD), F32)],
+        send, xsend, gsend,
+    )
 
 
 def exchange_tp(tsend):
-    mine = lax.psum_scatter(tsend, "tp", scatter_dimension=0, tiled=False)
-    return mine[0:6, 0:32].astype(BF16)
+    (trecv,) = remote(tp_kernel, "swap_tp", 2, [((TP, 8, 128), F32)], tsend)
+    return jnp.sum(trecv, axis=0)[0:6, 0:32].astype(BF16)
 
 
 def local(body, name, outs, scratch, *args):

time: 274 us -> 118 us (0.43)
  blocking collectives: 225 us -> 0 us
  Pallas kernels: 13.4 us -> 109 us
  starting transfers between devices: 23.9 us -> 0 us
    all_gather x2 -> x0, blocking collectives: 152 us -> none  [the longest x1 90.9 us: exchange_main(): return (recv, xrecv, lax.all_gather(gsend, 'seq', axis=0, tiled=False))]
    pallas_call x0 -> x3, Pallas kernels: none -> 97.6 us  [remote(): pl.pallas_call(body, name=name, out_shape=tuple((jax.ShapeDtypeStruct(s,...]
    unnamed x1 -> x0, blocking collectives: 51.1 us -> none
    all_to_all x2 -> x0, starting transfers between devices: 23.9 us -> none  [the longest x1 19.1 us: exchange_counts(): lax.all_to_all(rsend, 'seq', split_axis=0, concat_axis=0, tiled=True)]
    all_to_all x1 -> x0, blocking collectives: 22.1 us -> none  [exchange_main(): lax.all_to_all(xsend, 'seq', split_axis=0, concat_axis=0, tiled=True)]
    unnamed x20 -> x17, local copies, waits for them, and re-layouts: 5.98 us -> 4.71 us
  transfers between devices with their start and end apart: 2 -> 0, of which waited for: 0 -> 0; matrix products, arithmetic and copies ran while one was open for 1% -> 0% of each run, Pallas kernels for 0% -> 0%
where the time goes in v2:
time: 118 us; the launch traced here: 117 us
  Pallas kernels  109 us (92%)
  local copies, waits for them, and re-layouts  5.39 us (5%)
  other arithmetic  1.83 us (2%)
    pallas_call x3, Pallas kernels, remote(): pl.pallas_call(body, name=name, out_shape=tuple((jax.ShapeDtypeStruct(s,...  97.6 us
    pallas_call x4, Pallas kernels, local(): pl.pallas_call(body, name=name, out_shape=tuple((jax.ShapeDtypeStruct(s,...  11.8 us
    unnamed x17, local copies, waits for them, and re-layouts  4.71 us

profile of v2, /device:TPU:1, one launch (start us, length us, event | category | flops | bytes accessed | tf_op | source)
XLA Modules:
  0.0 117.3 jit_solution(8484748233917422708)
XLA Ops:
  0.6 0.7 pad_bitcast_fusion.req_ref
  1.3 0.0 copy-start
  1.3 1.2 %copy-done = bf16[2048,256]{1,0:T(8,128)(2,1)S(1)} copy-done((bf16[2048,256]{1,0:T(8,128)(2,1)S(1)}, bf16[2048,256]{1,0:T(8,128)(2,1)}, u32[]{:S(2)}) %copy-start) | copy-done | bytes 1048600
  2.5 0.0 copy-start.1
  2.5 1.2 %copy-done.1 = bf16[2048,256]{1,0:T(8,128)(2,1)S(1)} copy-done((bf16[2048,256]{1,0:T(8,128)(2,1)S(1)}, bf16[2048,256]{1,0:T(8,128)(2,1)}, u32[]{:S(2)}) %copy-start.1) | copy-done | bytes 1048600
  3.7 0.0 copy-start.2
  3.7 0.7 copy-done.2
  4.5 0.0 copy-start.5
  4.5 0.7 copy-done.5
  5.2 0.0 copy-start.6
  5.2 0.7 copy-done.6
  5.9 0.0 copy-start.3
  5.9 0.0 copy-start.4
  5.9 4.4 %pack.1 = (bf16[1040,512]{1,0:T(8,128)(2,1)S(1)}, s32[1,128]{1,0:T(1,128)S(1)}, f32[64,1,512]{2,1,0:T(1,128)S(1)}) custom-call(bf16[2048,256]{1,0:T(8,128)(2,1)S(1)} %copy-done, bf16[2048,256]{1,0:T(8,128)(2,1)S(1)} %copy-done.1, s32[16,128]{1,0:T(8,128)S(1)} %bitcast.5, s32[16,128]{1,0:T(8,128)S(1)} %bitcast.6, s32[1,128]{1,0:T(1,128)S(1)} %pad_bitcast_fusion.req_ref, ...), custom_call_target="tpu_custom_call" | custom-call | tf_op jit(solution)/shard_map/pack/pallas_call | solution.py:345
  10.3 24.8 %swap_counts.1 = (s32[64,1,128]{2,1,0:T(1,128)S(1)}, f32[64,1,512]{2,1,0:T(1,128)S(1)}) custom-call(s32[1,128]{1,0:T(1,128)S(1)} %get-tuple-element.20.counts, f32[64,1,512]{2,1,0:T(1,128)S(1)} %get-tuple-element.21.rsend), custom_call_target="tpu_custom_call" | custom-call | tf_op jit(solution)/shard_map/swap_counts/pallas_call | solution.py:259
  35.1 0.0 copy-done.3
  35.1 0.0 copy-done.4
  35.1 2.0 %turn.1 = (bf16[64,16,512]{2,1,0:T(8,128)(2,1)S(1)}, bf16[64,2,256]{2,1,0:T(2,128)(2,1)S(1)}, f32[1,256]{1,0:T(1,128)S(1)}) custom-call(s32[64,1,128]{2,1,0:T(1,128)S(1)} %get-tuple-element.22.counts, bf16[1040,512]{1,0:T(8,128)(2,1)S(1)} %get-tuple-element.23.grp, f32[64,1,512]{2,1,0:T(1,128)S(1)} %get-tuple-element.24.rrecv, ...), custom_call_target="tpu_custom_call" | custom-call | tf_op jit(solution)/shard_map/turn/pallas_call | solution.py:345
  37.1 0.0 copy-start.7
  37.1 64.2 %swap_main.1 = (bf16[64,16,512]{2,1,0:T(8,128)(2,1)S(1)}, bf16[64,2,256]{2,1,0:T(2,128)(2,1)S(1)}, f32[64,1,256]{2,1,0:T(1,128)S(1)}) custom-call(bf16[64,16,512]{2,1,0:T(8,128)(2,1)S(1)} %get-tuple-element.25.send, bf16[64,2,256]{2,1,0:T(2,128)(2,1)S(1)} %get-tuple-element.26.xsend, f32[1,256]{1,0:T(1,128)S(1)} %get-tuple-element.27.gsend), custom_call_target="tpu_custom_call" | custom-call | tf_op jit(solution)/shard_map/swap_main/pallas_call | solution.py:259
  101.3 4.9 %place.1 = (bf16[1040,256]{1,0:T(8,128)(2,1)}, bf16[1040,256]{1,0:T(8,128)(2,1)}, bf16[1,1040]{1,0:T(2,128)(2,1)S(1)}, s32[1,1040]{1,0:T(1,128)S(1)}) custom-call(s32[64,1,128]{2,1,0:T(1,128)S(1)} %get-tuple-element.22.counts, bf16[64,16,512]{2,1,0:T(8,128)(2,1)S(1)} %get-tuple-element.28.recv, bf16[64,2,256]{2,1,0:T(2,128)(2,1)S(1)} %get-tuple-element.29.xrecv, ...), custom_call_target="tpu_custom_call" | custom-call | tf_op jit(solution)/shard_map/place/pallas_call | solution.py:345
  106.2 0.6 reduce.1
  106.9 0.6 reduce
  107.5 0.0 copy-done.7
  107.5 0.1 copy.14
  107.6 0.5 project.1.tsend
  108.2 8.6 %swap_tp.1 = f32[8,8,128]{2,1,0:T(8,128)S(1)} custom-call(f32[8,8,128]{2,1,0:T(8,128)S(1)} %project.1.tsend), custom_call_target="tpu_custom_call" | custom-call | tf_op jit(solution)/shard_map/swap_tp/pallas_call | solution.py:259
  116.7 0.6 reduce_sum.9
  (1 shorter events, 0.0 us)
Async XLA Ops:
  1.3 1.2 %copy-start = (bf16[2048,256]{1,0:T(8,128)(2,1)S(1)}, bf16[2048,256]{1,0:T(8,128)(2,1)}, u32[]{:S(2)}) copy-start(bf16[2048,256]{1,0:T(8,128)(2,1)} %k_ref.1) | copy-start | bytes 3145732
  2.5 1.2 %copy-start.1 = (bf16[2048,256]{1,0:T(8,128)(2,1)S(1)}, bf16[2048,256]{1,0:T(8,128)(2,1)}, u32[]{:S(2)}) copy-start(bf16[2048,256]{1,0:T(8,128)(2,1)} %v_ref.1) | copy-start | bytes 3145732
  3.7 0.7 copy-start.2
  4.5 0.7 copy-start.5
  5.2 0.7 copy-start.6
  5.9 29.2 %copy-start.3 = (bf16[48,256]{1,0:T(8,128)(2,1)S(1)}, bf16[48,256]{1,0:T(8,128)(2,1)}, u32[]{:S(2)}) copy-start(bf16[48,256]{1,0:T(8,128)(2,1)} %nk_ref.1) | copy-start | bytes 73732
  5.9 29.2 %copy-start.4 = (bf16[48,256]{1,0:T(8,128)(2,1)S(1)}, bf16[48,256]{1,0:T(8,128)(2,1)}, u32[]{:S(2)}) copy-start(bf16[48,256]{1,0:T(8,128)(2,1)} %nv_ref.1) | copy-start | bytes 73732
  37.1 70.4 %copy-start.7 = (bf16[256,32]{0,1:T(8,128)(2,1)S(1)}, bf16[256,32]{0,1:T(8,128)(2,1)}, u32[]{:S(2)}) copy-start(bf16[256,32]{0,1:T(8,128)(2,1)} %param.17) | copy-start | bytes 49156

commit v3 on v1

--- a/solution.py
+++ b/solution.py
@@ -21,6 +21,7 @@
 TILE = 208
 TILES = K_DEV // TILE
 NEG = -1e30
+FIRST, SECOND = 24, 44
 
 
 def iota(shape, dim):
@@ -32,7 +33,8 @@
 
 
 def pack_kernel(
-    k_ref, v_ref, keep_ref, w_ref, req_ref, q_ref, grp, counts, rsend, part
+    k_ref, v_ref, keep_ref, w_ref, req_ref, q_ref, nk_ref, nv_ref,
+    twice, xtwice, counts, rsend, own_ref, grp, part, xf
 ):
     me = lax.axis_index("seq")
     keep = keep_ref[...]
@@ -75,6 +77,16 @@
         return 0
 
     lax.fori_loop(0, TILES, group, 0)
+    slabs = grp[0:MAIN, :].reshape(N, SLAB, 2 * HD)
+    twice[0:N] = slabs
+    twice[N : 2 * N] = slabs
+    xf[...] = grp[MAIN:K_DEV, :].astype(F32)
+    xtwice[...] = jnp.zeros(xtwice.shape, BF16)
+    for c in range(K_DEV - MAIN):
+        row = xf[c : c + 1, :]
+        pair = jnp.concatenate([row[:, 0:HD], row[:, HD : 2 * HD]], axis=0).astype(BF16)
+        xtwice[c] = pair
+        xtwice[N + c] = pair
 
     spread = spread_rows()
     q64 = jnp.dot(spread, q_ref[...], preferred_element_type=F32)
@@ -107,7 +119,15 @@
         rsend[s] = part[pl.ds(s, 1), :]
         return 0
 
-    lax.fori_loop(0, N, fill_part, 0)
+    lax.fori_loop(0, N, fill_part, 0, unroll=8)
+
+    mine = ((6 * (me >> 3) + (me & 7) == iota((8, REQS), 1)) & ((me & 7) < 6)).astype(BF16)
+    qr = jnp.dot(mine, q_ref[...], preferred_element_type=F32)
+    kr = jnp.dot(mine, nk_ref[...], preferred_element_type=F32)
+    nv = jnp.dot(mine, nv_ref[...], preferred_element_type=F32)[0:1, :]
+    own = jnp.sum(qr * kr, axis=1, keepdims=True)[0:1, :] * (1.0 / 16.0)
+    own_ref[:, 0:HD] = nv
+    own_ref[:, HD : HD + 128] = jnp.broadcast_to(own, (1, 128))
 
 
 def spread_rows():
@@ -123,62 +143,6 @@
     ends = jnp.sum(jnp.where(lane <= rid, req_row, 0.0), axis=1, keepdims=True)
     starts = jnp.sum(jnp.where(lane < rid, req_row, 0.0), axis=1, keepdims=True)
     return starts, ends
-
-
-def turn_kernel(counts, grp, rrecv, q_ref, nk_ref, nv_ref, send, xsend, gsend, xf):
-    me = lax.axis_index("seq")
-
-    def sum_before(s, carry):
-        return carry + jnp.where(s < me, counts[s], 0)
-
-    before = lax.fori_loop(0, N, sum_before, jnp.zeros((1, BLOCK), I32))
-    offset = jnp.sum(before)
-    xf[...] = grp[MAIN:K_DEV, :].astype(F32)
-
-    def turn(p, _):
-        c = (p - offset) & (N - 1)
-        send[p] = grp[pl.ds(pl.multiple_of(c * SLAB, SLAB), SLAB), :]
-        row = xf[pl.ds(c & 15, 1), :]
-        xsend[p] = jnp.concatenate([row[:, 0:HD], row[:, HD : 2 * HD]], axis=0).astype(BF16)
-        return 0
-
-    lax.fori_loop(0, N, turn, 0)
-
-    mine = ((6 * (me >> 3) + (me & 7) == iota((8, REQS), 1)) & ((me & 7) < 6)).astype(BF16)
-    qr = jnp.dot(mine, q_ref[...], preferred_element_type=F32)
-    kr = jnp.dot(mine, nk_ref[...], preferred_element_type=F32)
-    nv = jnp.dot(mine, nv_ref[...], preferred_element_type=F32)[0:1, :]
-    own = jnp.sum(qr * kr, axis=1, keepdims=True)[0:1, :] * (1.0 / 16.0)
-    own = jnp.broadcast_to(own, (1, 128))
-
-    def top(i, carry):
-        return jnp.maximum(carry, rrecv[i][:, HD : HD + 128])
-
-    peak = lax.fori_loop(0, N, top, own)
-
-    def merge(i, carry):
-        tot, wsum = carry
-        row = rrecv[i]
-        w = jnp.exp(row[:, HD : HD + 128] - peak)
-        tot = tot + w * row[:, HD + 128 : HD + 256]
-        wsum = wsum + jnp.concatenate([w, w], axis=1) * row[:, 0:HD]
-        return tot, wsum
-
-    own_p = jnp.exp(own - peak)
-    first = (own_p, jnp.concatenate([own_p, own_p], axis=1) * nv)
-    tot, wsum = lax.fori_loop(0, N, merge, first, unroll=8)
-    gsend[...] = (wsum / jnp.concatenate([tot, tot], axis=1)).astype(BF16).astype(F32)
-
-
-def project_kernel(grecv, ow_ref, tsend, a2):
-    def fill_rows(s, _):
-        a2[pl.ds(s, 1), :] = grecv[s]
-        return 0
-
-    lax.fori_loop(0, N, fill_rows, 0)
-    wide = jnp.dot(a2[...].astype(BF16), ow_ref[...], preferred_element_type=F32)
-    for p in range(TP):
-        tsend[p] = wide[8 * p : 8 * p + 8, :]
 
 
 def place_kernel(counts, recv, xrecv, req_ref, pk_ref, pv_ref, pb_ref, pr_ref, c2, x2, tgt):
@@ -254,20 +218,155 @@
     lax.fori_loop(0, TILES, place, 0)
 
 
-def exchange_counts(counts, rsend):
-    counts = lax.all_gather(counts, "seq", axis=0, tiled=False)
-    return counts, lax.all_to_all(rsend, "seq", split_axis=0, concat_axis=0, tiled=True)
-
-
-def exchange_main(send, xsend, gsend):
-    recv = lax.all_to_all(send, "seq", split_axis=0, concat_axis=0, tiled=True)
-    xrecv = lax.all_to_all(xsend, "seq", split_axis=0, concat_axis=0, tiled=True)
-    return recv, xrecv, lax.all_gather(gsend, "seq", axis=0, tiled=False)
-
-
-def exchange_tp(tsend):
-    mine = lax.psum_scatter(tsend, "tp", scatter_dimension=0, tiled=False)
-    return mine[0:6, 0:32].astype(BF16)
+def step_of(i):
+    half = (i + 1) // 2
+    return N // 2 + half * (1 - 2 * (i % 2))
+
+
+def swap_kernel(
+    counts, rsend, twice, xtwice, own_ref, ow_ref,
+    call, recv, xrecv, lo_ref,
+    send, xsend, rrecv, gsend, grecv, tsend, trecv,
+    s_c, r_c, s_p, r_p, s_m, r_m, s_x, r_x, s_g, r_g, s_t, r_t,
+):
+    me = lax.axis_index("seq")
+    mt = lax.axis_index("tp")
+
+    def seq_copy(src, dst, s_sem, r_sem, p):
+        return pltpu.make_async_remote_copy(
+            src, dst, s_sem, r_sem, device_id={"seq": p}, device_id_type=MESH
+        )
+
+    def tp_copy(src, dst, p):
+        return pltpu.make_async_remote_copy(
+            src, dst, s_t, r_t, device_id={"tp": p}, device_id_type=MESH
+        )
+
+    def partner(i):
+        return lax.rem(me + step_of(i), N)
+
+    barrier = pltpu.get_barrier_semaphore()
+
+    def greet(i, _):
+        pl.semaphore_signal(barrier, inc=1, device_id={"seq": partner(i)}, device_id_type=MESH)
+        return 0
+
+    lax.fori_loop(0, N - 1, greet, 0)
+
+    def greet_tp(i, _):
+        p = lax.rem(mt + 1 + i, TP)
+        pl.semaphore_signal(barrier, inc=1, device_id={"tp": p}, device_id_type=MESH)
+        return 0
+
+    lax.fori_loop(0, TP - 1, greet_tp, 0)
+    call[me] = counts[...]
+    rrecv[me] = rsend[me]
+    pl.semaphore_wait(barrier, N - 1 + TP - 1)
+
+    def send_counts(i, _):
+        seq_copy(counts, call.at[me], s_c, r_c, partner(i)).start()
+        return 0
+
+    lax.fori_loop(0, N - 1, send_counts, 0)
+
+    def send_part(i, _):
+        p = partner(i)
+        seq_copy(rsend.at[p], rrecv.at[me], s_p, r_p, p).start()
+        return 0
+
+    lax.fori_loop(0, N - 1, send_part, 0)
+
+    many = call.at[pl.ds(0, N - 1)]
+    seq_copy(many, many, s_c, r_c, lax.rem(me + 1, N)).wait_recv()
+    earlier = lax.broadcasted_iota(I32, (N, 1, BLOCK), 0) < me
+    offset = jnp.sum(jnp.sum(jnp.where(earlier, call[...], 0), axis=0))
+    turn = (0 - offset) & (N - 1)
+    send[...] = twice[pl.ds(turn, N)]
+    xsend[...] = xtwice[pl.ds(turn, N)]
+    recv[me] = send[me]
+    xrecv[me] = xsend[me]
+
+    def send_slab(i, _):
+        p = partner(i)
+        seq_copy(send.at[p], recv.at[me], s_m, r_m, p).start()
+        seq_copy(xsend.at[p], xrecv.at[me], s_x, r_x, p).start()
+        return 0
+
+    lax.fori_loop(0, FIRST, send_slab, 0)
+
+    many_p = rrecv.at[pl.ds(0, N - 1)]
+    seq_copy(many_p, many_p, s_p, r_p, lax.rem(me + 1, N)).wait_recv()
+    own = own_ref[:, HD : HD + 128]
+    peaks = rrecv[:, :, HD : HD + 128]
+    peak = jnp.maximum(jnp.max(peaks, axis=0), own)
+    w = jnp.exp(peaks - peak[None])
+    own_p = jnp.exp(own - peak)
+    tot = jnp.sum(w * rrecv[:, :, HD + 128 : HD + 256], axis=0) + own_p
+    for c in range(2):
+        lanes = slice(128 * c, 128 * (c + 1))
+        wsum = jnp.sum(w * rrecv[:, :, lanes], axis=0) + own_p * own_ref[:, lanes]
+        gsend[:, lanes] = (wsum / tot).astype(BF16).astype(F32)
+    grecv[me] = gsend[...]
+
+    def send_row(i, _):
+        seq_copy(gsend, grecv.at[me], s_g, r_g, partner(i)).start()
+        return 0
+
+    lax.fori_loop(0, N - 1, send_row, 0)
+    lax.fori_loop(FIRST, SECOND, send_slab, 0)
+
+    many_g = grecv.at[pl.ds(0, N - 1)]
+    seq_copy(many_g, many_g, s_g, r_g, lax.rem(me + 1, N)).wait_recv()
+    rows = grecv[...].reshape(N, HD).astype(BF16)
+    tsend[...] = jnp.dot(rows, ow_ref[...], preferred_element_type=F32).reshape(TP, 8, 128)
+    trecv[mt] = tsend[mt]
+
+    def send_tp(i, _):
+        p = lax.rem(mt + 1 + i, TP)
+        tp_copy(tsend.at[p], trecv.at[mt], p).start()
+        return 0
+
+    lax.fori_loop(0, TP - 1, send_tp, 0)
+    lax.fori_loop(SECOND, N - 1, send_slab, 0)
+
+    many_t = trecv.at[pl.ds(0, TP - 1)]
+    tp_copy(many_t, many_t, lax.rem(mt + 1, TP)).wait_recv()
+    lo_ref[...] = jnp.sum(trecv[...], axis=0)[0:6, 0:32].astype(BF16)
+
+    for buf, s_sem, r_sem in ((recv, s_m, r_m), (xrecv, s_x, r_x)):
+        many = buf.at[pl.ds(0, N - 1)]
+        seq_copy(many, many, s_sem, r_sem, lax.rem(me + 1, N)).wait_recv()
+    for buf, s_sem, r_sem in (
+        (call, s_c, r_c), (rrecv, s_p, r_p), (grecv, s_g, r_g), (recv, s_m, r_m), (xrecv, s_x, r_x)
+    ):
+        many = buf.at[pl.ds(0, N - 1)]
+        seq_copy(many, many, s_sem, r_sem, lax.rem(me + 1, N)).wait_send()
+    tp_copy(many_t, many_t, lax.rem(mt + 1, TP)).wait_send()
+
+
+def exchange(counts, rsend, twice, xtwice, own, ow):
+    vmem = pl.BlockSpec(memory_space=pltpu.VMEM)
+    outs = [((N, 1, BLOCK), I32), ((N, SLAB, 2 * HD), BF16), ((N, 2, HD), BF16), ((6, 32), BF16)]
+    scratch = [
+        ((N, SLAB, 2 * HD), BF16),
+        ((N, 2, HD), BF16),
+        ((N, 1, 2 * HD), F32),
+        ((1, HD), F32),
+        ((N, 1, HD), F32),
+        ((TP, 8, 128), F32),
+        ((TP, 8, 128), F32),
+    ]
+    return pl.pallas_call(
+        swap_kernel,
+        name="swap",
+        out_shape=tuple(jax.ShapeDtypeStruct(s, d) for s, d in outs),
+        in_specs=[vmem] * 6,
+        out_specs=(vmem,) * len(outs),
+        scratch_shapes=[pltpu.VMEM(s, d) for s, d in scratch] + [pltpu.SemaphoreType.DMA] * 12,
+        compiler_params=pltpu.CompilerParams(
+            collective_id=0, has_side_effects=True, vmem_limit_bytes=40 << 20
+        ),
+    )(counts, rsend, twice, xtwice, own, ow)
 
 
 def local(body, name, outs, scratch, *args):
@@ -288,22 +387,16 @@
     w2 = w.reshape(NB, BLOCK)
     req2 = jnp.pad(req, (0, BLOCK - REQS)).reshape(1, BLOCK)
     ow2 = jnp.pad(ow, ((0, 0), (0, 128 - ow.shape[1])))
-    grp, counts, rsend = local(
+    twice, xtwice, counts, rsend, own = local(
         pack_kernel, "pack",
-        [((K_DEV, 2 * HD), BF16), ((1, BLOCK), I32), ((N, 1, 2 * HD), F32)],
-        [((N, 2 * HD), F32)],
-        ck, cv, keep2, w2, req2, q,
-    )
-    counts, rrecv = exchange_counts(counts, rsend)
-    send, xsend, gsend = local(
-        turn_kernel, "turn",
-        [((N, SLAB, 2 * HD), BF16), ((N, 2, HD), BF16), ((1, HD), F32)],
-        [((16, 2 * HD), F32)],
-        counts, grp, rrecv, q, nk, nv,
-    )
-    recv, xrecv, grecv = exchange_main(send, xsend, gsend)
-    (tsend,) = local(project_kernel, "project", [((TP, 8, 128), F32)], [((N, HD), F32)], grecv, ow2)
-    lo = exchange_tp(tsend)
+        [
+            ((2 * N, SLAB, 2 * HD), BF16), ((2 * N, 2, HD), BF16), ((1, BLOCK), I32),
+            ((N, 1, 2 * HD), F32), ((1, HD + 128), F32),
+        ],
+        [((K_DEV, 2 * HD), BF16), ((N, 2 * HD), F32), ((K_DEV - MAIN, 2 * HD), F32)],
+        ck, cv, keep2, w2, req2, q, nk, nv,
+    )
+    counts, recv, xrecv, lo = exchange(counts, rsend, twice, xtwice, own, ow2)
     pk, pv, pb, pr = local(
         place_kernel, "place",
         [((K_DEV, HD), BF16), ((K_DEV, HD), BF16), ((1, K_DEV), BF16), ((1, K_DEV), I32)],

time: 274 us -> 98.7 us (0.36)
  blocking collectives: 225 us -> 0 us
  Pallas kernels: 13.4 us -> 88.2 us
  starting transfers between devices: 23.9 us -> 0 us
    all_gather x2 -> x0, blocking collectives: 152 us -> none  [the longest x1 90.9 us: exchange_main(): return (recv, xrecv, lax.all_gather(gsend, 'seq', axis=0, tiled=False))]
    pallas_call x0 -> x1, Pallas kernels: none -> 78.8 us  [exchange(): pl.pallas_call(swap_kernel, name='swap', out_shape=tuple((jax.ShapeDtypeS...]
    unnamed x1 -> x0, blocking collectives: 51.1 us -> none
    all_to_all x2 -> x0, starting transfers between devices: 23.9 us -> none  [the longest x1 19.1 us: exchange_counts(): lax.all_to_all(rsend, 'seq', split_axis=0, concat_axis=0, tiled=True)]
    all_to_all x1 -> x0, blocking collectives: 22.1 us -> none  [exchange_main(): lax.all_to_all(xsend, 'seq', split_axis=0, concat_axis=0, tiled=True)]
    pallas_call x4 -> x2, Pallas kernels: 13.4 us -> 9.39 us  [local(): pl.pallas_call(body, name=name, out_shape=tuple((jax.ShapeDtypeStruct(s,...]
    unnamed x20 -> x16, local copies, waits for them, and re-layouts: 5.98 us -> 7.46 us
  transfers between devices with their start and end apart: 2 -> 0, of which waited for: 0 -> 0; matrix products, arithmetic and copies ran while one was open for 1% -> 0% of each run, Pallas kernels for 0% -> 0%
where the time goes in v3:
time: 98.7 us; the launch traced here: 98.2 us
  Pallas kernels  88.2 us (89%)
  local copies, waits for them, and re-layouts  8.14 us (8%)
  other arithmetic  1.24 us (1%)
    pallas_call x1, Pallas kernels, exchange(): pl.pallas_call(swap_kernel, name='swap', out_shape=tuple((jax.ShapeDtypeS...  78.8 us
    pallas_call x2, Pallas kernels, local(): pl.pallas_call(body, name=name, out_shape=tuple((jax.ShapeDtypeStruct(s,...  9.39 us
    unnamed x16, local copies, waits for them, and re-layouts  7.46 us

profile of v3, /device:TPU:1, one launch (start us, length us, event | category | flops | bytes accessed | tf_op | source)
XLA Modules:
  0.0 98.2 jit_solution(7476532898490811092)
XLA Ops:
  0.6 0.7 pad_bitcast_fusion.req_ref
  1.3 0.8 copy.14
  2.2 0.0 copy-start
  2.2 1.2 %copy-done = bf16[2048,256]{1,0:T(8,128)(2,1)S(1)} copy-done((bf16[2048,256]{1,0:T(8,128)(2,1)S(1)}, bf16[2048,256]{1,0:T(8,128)(2,1)}, u32[]{:S(2)}) %copy-start) | copy-done | bytes 1048600
  3.4 0.0 copy-start.1
  3.4 1.2 %copy-done.1 = bf16[2048,256]{1,0:T(8,128)(2,1)S(1)} copy-done((bf16[2048,256]{1,0:T(8,128)(2,1)S(1)}, bf16[2048,256]{1,0:T(8,128)(2,1)}, u32[]{:S(2)}) %copy-start.1) | copy-done | bytes 1048600
  4.6 0.0 copy-start.2
  4.6 0.7 copy-done.2
  5.3 0.0 copy-start.3
  5.3 0.7 copy-done.3
  6.1 0.0 copy-start.4
  6.1 0.7 copy-done.4
  6.8 0.0 copy-start.5
  6.8 0.7 copy-done.5
  7.5 0.0 copy-start.6
  7.5 0.7 copy-done.6
  8.2 4.5 %pack.1 = (bf16[128,16,512]{2,1,0:T(8,128)(2,1)S(1)}, bf16[128,2,256]{2,1,0:T(2,128)(2,1)S(1)}, s32[1,128]{1,0:T(1,128)S(1)}, f32[64,1,512]{2,1,0:T(1,128)S(1)}, f32[1,384]{1,0:T(1,128)S(1)}) custom-call(bf16[2048,256]{1,0:T(8,128)(2,1)S(1)} %copy-done, bf16[2048,256]{1,0:T(8,128)(2,1)S(1)} %copy-done.1, s32[16,128]{1,0:T(8,128)S(1)} %bitcast.4, ...), custom_call_target="tpu_custom_call" | custom-call | tf_op jit(solution)/shard_map/pack/pallas_call | solution.py:374
  12.7 78.8 %swap.1 = (s32[64,1,128]{2,1,0:T(1,128)S(1)}, bf16[64,16,512]{2,1,0:T(8,128)(2,1)S(1)}, bf16[64,2,256]{2,1,0:T(2,128)(2,1)S(1)}, bf16[6,32]{1,0:T(8,128)(2,1)S(1)}) custom-call(s32[1,128]{1,0:T(1,128)S(1)} %get-tuple-element.18.counts, f32[64,1,512]{2,1,0:T(1,128)S(1)} %get-tuple-element.19.rsend, bf16[128,16,512]{2,1,0:T(8,128)(2,1)S(1)} %get-tuple-element.20.twice, ...), custom_call_target="tpu_custom_call" | custom-call | tf_op jit(solution)/shard_map/swap/pallas_call | solution.py:359
  91.5 4.9 %place.1 = (bf16[1040,256]{1,0:T(8,128)(2,1)}, bf16[1040,256]{1,0:T(8,128)(2,1)}, bf16[1,1040]{1,0:T(2,128)(2,1)S(1)}, s32[1,1040]{1,0:T(1,128)S(1)}) custom-call(s32[64,1,128]{2,1,0:T(1,128)S(1)} %get-tuple-element.23.counts, bf16[64,16,512]{2,1,0:T(8,128)(2,1)S(1)} %get-tuple-element.24.recv, bf16[64,2,256]{2,1,0:T(2,128)(2,1)S(1)} %get-tuple-element.25.xrecv, ...), custom_call_target="tpu_custom_call" | custom-call | tf_op jit(solution)/shard_map/place/pallas_call | solution.py:374
  96.4 0.6 reduce
  97.0 0.6 reduce.1
  97.6 0.6 copy.16
  (1 shorter events, 0.0 us)
Async XLA Ops:
  2.2 1.2 %copy-start = (bf16[2048,256]{1,0:T(8,128)(2,1)S(1)}, bf16[2048,256]{1,0:T(8,128)(2,1)}, u32[]{:S(2)}) copy-start(bf16[2048,256]{1,0:T(8,128)(2,1)} %k_ref.1) | copy-start | bytes 3145732
  3.4 1.2 %copy-start.1 = (bf16[2048,256]{1,0:T(8,128)(2,1)S(1)}, bf16[2048,256]{1,0:T(8,128)(2,1)}, u32[]{:S(2)}) copy-start(bf16[2048,256]{1,0:T(8,128)(2,1)} %v_ref.1) | copy-start | bytes 3145732
  4.6 0.7 copy-start.2
  5.3 0.7 copy-start.3
  6.1 0.7 copy-start.4
  6.8 0.7 copy-start.5
  7.5 0.7 copy-start.6

commit v4 on v3

--- a/solution.py
+++ b/solution.py
@@ -21,7 +21,9 @@
 TILE = 208
 TILES = K_DEV // TILE
 NEG = -1e30
-FIRST, SECOND = 24, 44
+NX = 4
+NZ = N // NX
+CUTS = (0, 12, 24, 36, 48, N - 1)
 
 
 def iota(shape, dim):
@@ -116,12 +118,14 @@
     part[:, HD + 128 : HD + 256] = jnp.broadcast_to(total, (N, 128))
 
     def fill_part(s, _):
-        rsend[s] = part[pl.ds(s, 1), :]
-        return 0
-
-    lax.fori_loop(0, N, fill_part, 0, unroll=8)
-
-    mine = ((6 * (me >> 3) + (me & 7) == iota((8, REQS), 1)) & ((me & 7) < 6)).astype(BF16)
+        for x in range(NX):
+            rsend[x, s] = part[pl.ds(x * NZ + s, 1), :]
+        return 0
+
+    lax.fori_loop(0, NZ, fill_part, 0)
+
+    row = (me & (NX - 1)) * NZ + (me >> 2)
+    mine = ((6 * (row >> 3) + (row & 7) == iota((8, REQS), 1)) & ((row & 7) < 6)).astype(BF16)
     qr = jnp.dot(mine, q_ref[...], preferred_element_type=F32)
     kr = jnp.dot(mine, nk_ref[...], preferred_element_type=F32)
     nv = jnp.dot(mine, nv_ref[...], preferred_element_type=F32)[0:1, :]
@@ -136,8 +140,8 @@
 
 
 def request_blocks(req_ref):
-    srow = iota((N, BLOCK), 0)
-    lane = iota((N, BLOCK), 1)
+    srow = iota((N, REQS), 0)
+    lane = iota((N, REQS), 1)
     rid = 6 * (srow >> 3) + (srow & 7)
     req_row = req_ref[...].astype(F32)
     ends = jnp.sum(jnp.where(lane <= rid, req_row, 0.0), axis=1, keepdims=True)
@@ -145,18 +149,11 @@
     return starts, ends
 
 
-def place_kernel(counts, recv, xrecv, req_ref, pk_ref, pv_ref, pb_ref, pr_ref, c2, x2, tgt):
-    me = lax.axis_index("seq")
+def slot_tables(call, req_ref, me, pb_ref, pr_ref, tgt, xtgt):
     srow = iota((N, BLOCK), 0)
     lane = iota((N, BLOCK), 1)
     _, ends = request_blocks(req_ref)
-
-    def fill_counts(s, _):
-        c2[pl.ds(s, 1), :] = counts[s]
-        return 0
-
-    lax.fori_loop(0, N, fill_counts, 0)
-    sizes = c2[...].astype(F32)
+    sizes = call[...].reshape(N, BLOCK).astype(F32)
     sizes16 = sizes.astype(BF16)
     n_col = jnp.sum(sizes, axis=1, keepdims=True)
     before64 = (iota((N, N), 1) < iota((N, N), 0)).astype(BF16)
@@ -193,7 +190,10 @@
     is_src = srow == lane
     k0 = jnp.sum(jnp.where(is_src, k0_col, 0.0), axis=0, keepdims=True)
     lim = jnp.sum(jnp.where(is_src, lim_col, 0.0), axis=0, keepdims=True)
-    xtgt = jnp.where(lim > float(MAIN), k0 + float(SLAB), -1.0).astype(I32)
+    xtgt[...] = jnp.where(lim > float(MAIN), k0 + float(SLAB), -1.0).astype(I32)
+
+
+def place_kernel(recv, xrecv, tgt, xtgt, pk_ref, pv_ref, x2):
     x2[...] = jnp.zeros(x2.shape, F32)
 
     def fill_extra(i, _):
@@ -202,12 +202,12 @@
         x2[pl.ds(i, 1), HD : 2 * HD] = pair[1:2, :]
         return 0
 
-    lax.fori_loop(0, N, fill_extra, 0)
+    lax.fori_loop(0, N, fill_extra, 0, unroll=8)
 
     def place(j, _):
         start = pl.multiple_of(j * TILE, 16)
         sel = jnp.where(iota((TILE, MAIN), 0) + start == tgt[...], 1.0, 0.0).astype(BF16)
-        xsel = jnp.where(iota((TILE, BLOCK), 0) + start == xtgt, 1.0, 0.0).astype(BF16)
+        xsel = jnp.where(iota((TILE, BLOCK), 0) + start == xtgt[...], 1.0, 0.0).astype(BF16)
         rows = recv[...].reshape(MAIN, 2 * HD)
         got = jnp.dot(sel, rows, preferred_element_type=F32)
         got = got + jnp.dot(xsel, x2[...].astype(BF16), preferred_element_type=F32)
@@ -224,13 +224,14 @@
 
 
 def swap_kernel(
-    counts, rsend, twice, xtwice, own_ref, ow_ref,
-    call, recv, xrecv, lo_ref,
-    send, xsend, rrecv, gsend, grecv, tsend, trecv,
-    s_c, r_c, s_p, r_p, s_m, r_m, s_x, r_x, s_g, r_g, s_t, r_t,
+    counts, rsend, twice, xtwice, own_ref, ow_ref, req_ref,
+    recv, xrecv, lo_ref, pb_ref, pr_ref, tgt, xtgt,
+    call, send, xsend, prow, zsend, pcol, gsend, grecv, tsend, trecv,
+    s_c, r_c, s_p, r_p, s_q, r_q, s_m, r_m, s_x, r_x, s_g, r_g, s_h, r_h, s_t, r_t,
 ):
     me = lax.axis_index("seq")
     mt = lax.axis_index("tp")
+    z, x = lax.div(me, NX), lax.rem(me, NX)
 
     def seq_copy(src, dst, s_sem, r_sem, p):
         return pltpu.make_async_remote_copy(
@@ -245,6 +246,13 @@
     def partner(i):
         return lax.rem(me + step_of(i), N)
 
+    def z_part(i):
+        return lax.rem(z + 1 + i, NZ)
+
+    def x_part(i):
+        return lax.rem(x + 1 + i, NX)
+
+    near = lax.rem(me + 1, N)
     barrier = pltpu.get_barrier_semaphore()
 
     def greet(i, _):
@@ -260,7 +268,7 @@
 
     lax.fori_loop(0, TP - 1, greet_tp, 0)
     call[me] = counts[...]
-    rrecv[me] = rsend[me]
+    prow[x] = rsend[x]
     pl.semaphore_wait(barrier, N - 1 + TP - 1)
 
     def send_counts(i, _):
@@ -270,21 +278,19 @@
     lax.fori_loop(0, N - 1, send_counts, 0)
 
     def send_part(i, _):
-        p = partner(i)
-        seq_copy(rsend.at[p], rrecv.at[me], s_p, r_p, p).start()
-        return 0
-
-    lax.fori_loop(0, N - 1, send_part, 0)
-
-    many = call.at[pl.ds(0, N - 1)]
-    seq_copy(many, many, s_c, r_c, lax.rem(me + 1, N)).wait_recv()
+        p = x_part(i)
+        seq_copy(rsend.at[p], prow.at[x], s_p, r_p, z * NX + p).start()
+        return 0
+
+    lax.fori_loop(0, NX - 1, send_part, 0)
+
+    all_c = call.at[pl.ds(0, N - 1)]
+    seq_copy(all_c, all_c, s_c, r_c, near).wait_recv()
     earlier = lax.broadcasted_iota(I32, (N, 1, BLOCK), 0) < me
     offset = jnp.sum(jnp.sum(jnp.where(earlier, call[...], 0), axis=0))
     turn = (0 - offset) & (N - 1)
     send[...] = twice[pl.ds(turn, N)]
     xsend[...] = xtwice[pl.ds(turn, N)]
-    recv[me] = send[me]
-    xrecv[me] = xsend[me]
 
     def send_slab(i, _):
         p = partner(i)
@@ -292,33 +298,66 @@
         seq_copy(xsend.at[p], xrecv.at[me], s_x, r_x, p).start()
         return 0
 
-    lax.fori_loop(0, FIRST, send_slab, 0)
-
-    many_p = rrecv.at[pl.ds(0, N - 1)]
-    seq_copy(many_p, many_p, s_p, r_p, lax.rem(me + 1, N)).wait_recv()
+    lax.fori_loop(CUTS[0], CUTS[1], send_slab, 0)
+    recv[me] = send[me]
+    xrecv[me] = xsend[me]
+
+    all_p = prow.at[pl.ds(0, NX - 1)]
+    seq_copy(all_p, all_p, s_p, r_p, near).wait_recv()
+    peaks = prow[:, :, :, HD : HD + 128]
+    peak = jnp.max(peaks, axis=0)
+    w = jnp.exp(peaks - peak[None])
+    for c in (0, 1, 3):
+        lanes = slice(128 * c, 128 * (c + 1))
+        zsend[:, :, lanes] = jnp.sum(w * prow[:, :, :, lanes], axis=0)
+    zsend[:, :, HD : HD + 128] = peak
+    pcol[z] = zsend[z]
+
+    def send_merged(i, _):
+        p = z_part(i)
+        seq_copy(zsend.at[p], pcol.at[z], s_q, r_q, p * NX + x).start()
+        return 0
+
+    lax.fori_loop(0, NZ - 1, send_merged, 0)
+    lax.fori_loop(CUTS[1], CUTS[2], send_slab, 0)
+
+    all_q = pcol.at[pl.ds(0, NZ - 1)]
+    seq_copy(all_q, all_q, s_q, r_q, near).wait_recv()
     own = own_ref[:, HD : HD + 128]
-    peaks = rrecv[:, :, HD : HD + 128]
+    peaks = pcol[:, :, HD : HD + 128]
     peak = jnp.maximum(jnp.max(peaks, axis=0), own)
     w = jnp.exp(peaks - peak[None])
     own_p = jnp.exp(own - peak)
-    tot = jnp.sum(w * rrecv[:, :, HD + 128 : HD + 256], axis=0) + own_p
+    tot = jnp.sum(w * pcol[:, :, HD + 128 : HD + 256], axis=0) + own_p
     for c in range(2):
         lanes = slice(128 * c, 128 * (c + 1))
-        wsum = jnp.sum(w * rrecv[:, :, lanes], axis=0) + own_p * own_ref[:, lanes]
+        wsum = jnp.sum(w * pcol[:, :, lanes], axis=0) + own_p * own_ref[:, lanes]
         gsend[:, lanes] = (wsum / tot).astype(BF16).astype(F32)
-    grecv[me] = gsend[...]
+    grecv[x, z] = gsend[...]
 
     def send_row(i, _):
-        seq_copy(gsend, grecv.at[me], s_g, r_g, partner(i)).start()
-        return 0
-
-    lax.fori_loop(0, N - 1, send_row, 0)
-    lax.fori_loop(FIRST, SECOND, send_slab, 0)
-
-    many_g = grecv.at[pl.ds(0, N - 1)]
-    seq_copy(many_g, many_g, s_g, r_g, lax.rem(me + 1, N)).wait_recv()
+        seq_copy(gsend, grecv.at[x, z], s_g, r_g, z_part(i) * NX + x).start()
+        return 0
+
+    lax.fori_loop(0, NZ - 1, send_row, 0)
+    lax.fori_loop(CUTS[2], CUTS[3], send_slab, 0)
+
+    all_g = grecv.at[0, pl.ds(0, NZ - 1)]
+    seq_copy(all_g, all_g, s_g, r_g, near).wait_recv()
+
+    def send_rows(i, _):
+        seq_copy(grecv.at[x], grecv.at[x], s_h, r_h, z * NX + x_part(i)).start()
+        return 0
+
+    lax.fori_loop(0, NX - 1, send_rows, 0)
+    lax.fori_loop(CUTS[3], CUTS[4], send_slab, 0)
+
+    all_h = grecv.at[pl.ds(0, NX - 1)]
+    seq_copy(all_h, all_h, s_h, r_h, near).wait_recv()
     rows = grecv[...].reshape(N, HD).astype(BF16)
-    tsend[...] = jnp.dot(rows, ow_ref[...], preferred_element_type=F32).reshape(TP, 8, 128)
+    wide = lax.dot_general(rows, ow_ref[...], (((1,), (1,)), ((), ())), preferred_element_type=F32)
+    wide = jnp.concatenate([wide, jnp.zeros((N, 96), F32)], axis=1)
+    tsend[...] = wide.reshape(TP, 8, 128)
     trecv[mt] = tsend[mt]
 
     def send_tp(i, _):
@@ -327,32 +366,40 @@
         return 0
 
     lax.fori_loop(0, TP - 1, send_tp, 0)
-    lax.fori_loop(SECOND, N - 1, send_slab, 0)
-
-    many_t = trecv.at[pl.ds(0, TP - 1)]
-    tp_copy(many_t, many_t, lax.rem(mt + 1, TP)).wait_recv()
+    lax.fori_loop(CUTS[4], CUTS[5], send_slab, 0)
+    slot_tables(call, req_ref, me, pb_ref, pr_ref, tgt, xtgt)
+
+    all_t = trecv.at[pl.ds(0, TP - 1)]
+    tp_copy(all_t, all_t, lax.rem(mt + 1, TP)).wait_recv()
     lo_ref[...] = jnp.sum(trecv[...], axis=0)[0:6, 0:32].astype(BF16)
 
-    for buf, s_sem, r_sem in ((recv, s_m, r_m), (xrecv, s_x, r_x)):
-        many = buf.at[pl.ds(0, N - 1)]
-        seq_copy(many, many, s_sem, r_sem, lax.rem(me + 1, N)).wait_recv()
-    for buf, s_sem, r_sem in (
-        (call, s_c, r_c), (rrecv, s_p, r_p), (grecv, s_g, r_g), (recv, s_m, r_m), (xrecv, s_x, r_x)
+    all_m = recv.at[pl.ds(0, N - 1)]
+    all_x = xrecv.at[pl.ds(0, N - 1)]
+    for part, s_sem, r_sem in ((all_m, s_m, r_m), (all_x, s_x, r_x)):
+        seq_copy(part, part, s_sem, r_sem, near).wait_recv()
+    for part, s_sem, r_sem in (
+        (all_c, s_c, r_c), (all_p, s_p, r_p), (all_q, s_q, r_q), (all_g, s_g, r_g),
+        (all_h, s_h, r_h), (all_m, s_m, r_m), (all_x, s_x, r_x),
     ):
-        many = buf.at[pl.ds(0, N - 1)]
-        seq_copy(many, many, s_sem, r_sem, lax.rem(me + 1, N)).wait_send()
-    tp_copy(many_t, many_t, lax.rem(mt + 1, TP)).wait_send()
-
-
-def exchange(counts, rsend, twice, xtwice, own, ow):
+        seq_copy(part, part, s_sem, r_sem, near).wait_send()
+    tp_copy(all_t, all_t, lax.rem(mt + 1, TP)).wait_send()
+
+
+def exchange(counts, rsend, twice, xtwice, own, ow, req):
     vmem = pl.BlockSpec(memory_space=pltpu.VMEM)
-    outs = [((N, 1, BLOCK), I32), ((N, SLAB, 2 * HD), BF16), ((N, 2, HD), BF16), ((6, 32), BF16)]
+    outs = [
+        ((N, SLAB, 2 * HD), BF16), ((N, 2, HD), BF16), ((6, 32), BF16),
+        ((1, K_DEV), BF16), ((1, K_DEV), I32), ((1, MAIN), I32), ((1, BLOCK), I32),
+    ]
     scratch = [
+        ((N, 1, BLOCK), I32),
         ((N, SLAB, 2 * HD), BF16),
         ((N, 2, HD), BF16),
-        ((N, 1, 2 * HD), F32),
+        ((NX, NZ, 1, 2 * HD), F32),
+        ((NZ, 1, 2 * HD), F32),
+        ((NZ, 1, 2 * HD), F32),
         ((1, HD), F32),
-        ((N, 1, HD), F32),
+        ((NX, NZ, 1, HD), F32),
         ((TP, 8, 128), F32),
         ((TP, 8, 128), F32),
     ]
@@ -360,48 +407,53 @@
         swap_kernel,
         name="swap",
         out_shape=tuple(jax.ShapeDtypeStruct(s, d) for s, d in outs),
-        in_specs=[vmem] * 6,
+        in_specs=[vmem] * 7,
         out_specs=(vmem,) * len(outs),
-        scratch_shapes=[pltpu.VMEM(s, d) for s, d in scratch] + [pltpu.SemaphoreType.DMA] * 12,
+        scratch_shapes=[pltpu.VMEM(s, d) for s, d in scratch] + [pltpu.SemaphoreType.DMA] * 16,
         compiler_params=pltpu.CompilerParams(
             collective_id=0, has_side_effects=True, vmem_limit_bytes=40 << 20
         ),
-    )(counts, rsend, twice, xtwice, own, ow)
-
-
-def local(body, name, outs, scratch, *args):
+    )(counts, rsend, twice, xtwice, own, ow, req)
+
+
+def local(body, name, outs, scratch, *args, fetch=False):
     vmem = pl.BlockSpec(memory_space=pltpu.VMEM)
+    whole = {"in_specs": [vmem] * len(args)}
+    if fetch:
+        whole = {
+            "grid": (1,),
+            "in_specs": [pl.BlockSpec(a.shape, lambda i: (0, 0)) for a in args],
+        }
     return pl.pallas_call(
         body,
         name=name,
         out_shape=tuple(jax.ShapeDtypeStruct(s, d) for s, d in outs),
-        in_specs=[vmem] * len(args),
         out_specs=(vmem,) * len(outs),
         scratch_shapes=[pltpu.VMEM(s, d) for s, d in scratch],
         compiler_params=pltpu.CompilerParams(vmem_limit_bytes=40 << 20),
+        **whole,
     )(*args)
 
 
 def on_device(ck, cv, keep, w, req, q, nk, nv, ow):
     keep2 = keep.reshape(NB, BLOCK)
     w2 = w.reshape(NB, BLOCK)
-    req2 = jnp.pad(req, (0, BLOCK - REQS)).reshape(1, BLOCK)
-    ow2 = jnp.pad(ow, ((0, 0), (0, 128 - ow.shape[1])))
+    req2 = req.reshape(1, REQS)
     twice, xtwice, counts, rsend, own = local(
         pack_kernel, "pack",
         [
             ((2 * N, SLAB, 2 * HD), BF16), ((2 * N, 2, HD), BF16), ((1, BLOCK), I32),
-            ((N, 1, 2 * HD), F32), ((1, HD + 128), F32),
+            ((NX, NZ, 1, 2 * HD), F32), ((1, HD + 128), F32),
         ],
         [((K_DEV, 2 * HD), BF16), ((N, 2 * HD), F32), ((K_DEV - MAIN, 2 * HD), F32)],
         ck, cv, keep2, w2, req2, q, nk, nv,
-    )
-    counts, recv, xrecv, lo = exchange(counts, rsend, twice, xtwice, own, ow2)
-    pk, pv, pb, pr = local(
+        fetch=True,
+    )
+    recv, xrecv, lo, pb, pr, tgt, xtgt = exchange(counts, rsend, twice, xtwice, own, ow.T, req2)
+    pk, pv = local(
         place_kernel, "place",
-        [((K_DEV, HD), BF16), ((K_DEV, HD), BF16), ((1, K_DEV), BF16), ((1, K_DEV), I32)],
-        [((N, BLOCK), I32), ((BLOCK, 2 * HD), F32), ((1, MAIN), I32)],
-        counts, recv, xrecv, req2,
+        [((K_DEV, HD), BF16), ((K_DEV, HD), BF16)], [((BLOCK, 2 * HD), F32)],
+        recv, xrecv, tgt, xtgt,
     )
     return pk, pv, pb.reshape(K_DEV), pr.reshape(K_DEV), lo
 

time: 98.7 us -> 95.2 us (0.965)
  Pallas kernels: 88.2 us -> 85.5 us
    pallas_call x2, Pallas kernels: 9.39 us -> 7.87 us  [local(): pl.pallas_call(body, name=name, out_shape=tuple((jax.ShapeDtypeStruct(s,...]
    pallas_call x1, Pallas kernels: 78.8 us -> 77.6 us  [exchange(): pl.pallas_call(swap_kernel, name='swap', out_shape=tuple((jax.ShapeDtypeS...]
    unnamed x16 -> x19, local copies, waits for them, and re-layouts: 7.46 us -> 7.28 us
where the time goes in v4:
time: 95.2 us; the launch traced here: 94.7 us
  Pallas kernels  85.5 us (90%)
  local copies, waits for them, and re-layouts  7.28 us (8%)
  other arithmetic  1.24 us (1%)
    pallas_call x1, Pallas kernels, exchange(): pl.pallas_call(swap_kernel, name='swap', out_shape=tuple((jax.ShapeDtypeS...  77.6 us
    pallas_call x2, Pallas kernels, local(): pl.pallas_call(body, name=name, out_shape=tuple((jax.ShapeDtypeStruct(s,...  7.87 us
    unnamed x19, local copies, waits for them, and re-layouts  7.28 us

profile of v4, /device:TPU:1, one launch (start us, length us, event | category | flops | bytes accessed | tf_op | source)
XLA Modules:
  0.0 94.7 jit_solution(8643990209555868747)
XLA Ops:
  0.6 0.0 copy-start
  0.6 1.2 %copy-done = bf16[2048,256]{1,0:T(8,128)(2,1)S(1)} copy-done((bf16[2048,256]{1,0:T(8,128)(2,1)S(1)}, bf16[2048,256]{1,0:T(8,128)(2,1)}, u32[]{:S(2)}) %copy-start) | copy-done | bytes 1048600
  1.9 0.0 copy-start.1
  1.9 1.2 %copy-done.1 = bf16[2048,256]{1,0:T(8,128)(2,1)S(1)} copy-done((bf16[2048,256]{1,0:T(8,128)(2,1)S(1)}, bf16[2048,256]{1,0:T(8,128)(2,1)}, u32[]{:S(2)}) %copy-start.1) | copy-done | bytes 1048600
  3.1 0.0 copy-start.2
  3.1 0.7 copy-done.2
  3.8 0.0 copy-start.3
  3.8 0.7 copy-done.3
  4.6 0.0 copy-start.4
  4.6 0.7 copy-done.4
  5.3 0.0 copy-start.6
  5.3 0.7 copy-done.6
  6.0 0.0 copy-start.7
  6.0 0.7 copy-done.7
  6.7 0.0 copy-start.8
  6.7 0.7 copy-done.8
  7.3 0.0 copy-start.5
  7.4 4.5 %pack.1 = (bf16[128,16,512]{2,1,0:T(8,128)(2,1)S(1)}, bf16[128,2,256]{2,1,0:T(2,128)(2,1)S(1)}, s32[1,128]{1,0:T(1,128)S(1)}, f32[4,16,1,512]{3,2,1,0:T(1,128)S(1)}, f32[1,384]{1,0:T(1,128)S(1)}) custom-call(bf16[2048,256]{1,0:T(8,128)(2,1)S(1)} %copy-done, bf16[2048,256]{1,0:T(8,128)(2,1)S(1)} %copy-done.1, s32[16,128]{1,0:T(8,128)S(1)} %bitcast.5, ...), custom_call_target="tpu_custom_call" | custom-call | tf_op jit(solution)/shard_map/pack/pallas_call | solution.py:427
  11.9 0.0 copy-done.5
  11.9 77.6 %swap.1 = (bf16[64,16,512]{2,1,0:T(8,128)(2,1)S(1)}, bf16[64,2,256]{2,1,0:T(2,128)(2,1)S(1)}, bf16[6,32]{1,0:T(8,128)(2,1)S(1)}, bf16[1,1040]{1,0:T(2,128)(2,1)S...) custom-call(s32[1,128]{1,0:T(1,128)S(1)} %get-tuple-element.19.counts, ...), custom_call_target="tpu_custom_call" | custom-call | tf_op jit(solution)/shard_map/swap/pallas_call | solution.py:406
  89.5 3.4 %place.1 = (bf16[1040,256]{1,0:T(8,128)(2,1)}, bf16[1040,256]{1,0:T(8,128)(2,1)}) custom-call(bf16[64,16,512]{2,1,0:T(8,128)(2,1)S(1)} %get-tuple-element.24.recv, bf16[64,2,256]{2,1,0:T(2,128)(2,1)S(1)} %get-tuple-element.25.xrecv, s32[1,1024]{1,0:T(1,128)S(1)} %get-tuple-element.26.tgt, s32[1,128]{1,0:T(1,128)S(1)} %get-tuple-element.27.xtgt), custom_call_target="tpu_custom_call" | custom-call | tf_op jit(solution)/shard_map/place/pallas_call | solution.py:427
  92.9 0.6 reduce
  93.5 0.6 reduce.1
  94.1 0.6 copy.15
Async XLA Ops:
  0.6 1.2 %copy-start = (bf16[2048,256]{1,0:T(8,128)(2,1)S(1)}, bf16[2048,256]{1,0:T(8,128)(2,1)}, u32[]{:S(2)}) copy-start(bf16[2048,256]{1,0:T(8,128)(2,1)} %k_ref.1) | copy-start | bytes 3145732
  1.9 1.2 %copy-start.1 = (bf16[2048,256]{1,0:T(8,128)(2,1)S(1)}, bf16[2048,256]{1,0:T(8,128)(2,1)}, u32[]{:S(2)}) copy-start(bf16[2048,256]{1,0:T(8,128)(2,1)} %v_ref.1) | copy-start | bytes 3145732
  3.1 0.7 copy-start.2
  3.8 0.7 copy-start.3
  4.6 0.7 copy-start.4
  5.3 0.7 copy-start.6
  6.0 0.7 copy-start.7
  6.7 0.7 copy-start.8
  7.3 4.5 %copy-start.5 = (bf16[256,32]{0,1:T(8,128)(2,1)S(1)}, bf16[256,32]{0,1:T(8,128)(2,1)}, u32[]{:S(2)}) copy-start(bf16[256,32]{0,1:T(8,128)(2,1)} %param.17) | copy-start | bytes 49156

commit v5 on v4

--- a/solution.py
+++ b/solution.py
@@ -167,7 +167,7 @@
     for b in range(NB):
         hit = (block_end[:, b : b + 1] - 1.0) == j_row
         bias_out = jnp.where(hit, logs[:, b : b + 1], bias_out)
-    pb_ref[...] = jnp.sum(bias_out, axis=0, keepdims=True).astype(BF16)
+    pb_ref[...] = jnp.sum(bias_out, axis=0).astype(BF16)
     last = ends.astype(I32) - 1
     pick = (iota((N, N), 1) == (last >> 4)).astype(F32)
     picked = jnp.dot(pick, block_end, preferred_element_type=F32, precision=lax.Precision.HIGHEST)
@@ -175,7 +175,7 @@
     past = ((req_end <= j_row) & ((iota((N, K_DEV), 0) & 7) < 6)).astype(F32)
     owner = jnp.sum(past, axis=0, keepdims=True)
     every = jnp.sum(n_col, axis=0, keepdims=True)
-    pr_ref[...] = jnp.where(j_row < every, owner, -1.0).astype(I32)
+    pr_ref[...] = jnp.where(j_row < every, owner, -1.0).astype(I32)[0]
 
     off_i = off_col.astype(I32)
     c_col = (me - off_i) & (N - 1)
@@ -389,7 +389,7 @@
     vmem = pl.BlockSpec(memory_space=pltpu.VMEM)
     outs = [
         ((N, SLAB, 2 * HD), BF16), ((N, 2, HD), BF16), ((6, 32), BF16),
-        ((1, K_DEV), BF16), ((1, K_DEV), I32), ((1, MAIN), I32), ((1, BLOCK), I32),
+        ((K_DEV,), BF16), ((K_DEV,), I32), ((1, MAIN), I32), ((1, BLOCK), I32),
     ]
     scratch = [
         ((N, 1, BLOCK), I32),
@@ -420,6 +420,7 @@
     vmem = pl.BlockSpec(memory_space=pltpu.VMEM)
     whole = {"in_specs": [vmem] * len(args)}
     if fetch:
+        args = [pltpu.with_memory_space_constraint(a, pltpu.HBM) for a in args]
         whole = {
             "grid": (1,),
             "in_specs": [pl.BlockSpec(a.shape, lambda i: (0, 0)) for a in args],
@@ -455,7 +456,7 @@
         [((K_DEV, HD), BF16), ((K_DEV, HD), BF16)], [((BLOCK, 2 * HD), F32)],
         recv, xrecv, tgt, xtgt,
     )
-    return pk, pv, pb.reshape(K_DEV), pr.reshape(K_DEV), lo
+    return pk, pv, pb, pr, lo
 
 
 def solution(mesh):

time: 95.2 us -> 89.8 us (0.943)
  local copies, waits for them, and re-layouts: 7.28 us -> 1.78 us
  Pallas kernels: 85.5 us -> 87.2 us
  other arithmetic: 1.24 us -> 0 us
    unnamed x19 -> x7, local copies, waits for them, and re-layouts: 7.28 us -> 1.78 us
    pallas_call x2, Pallas kernels: 7.87 us -> 9.45 us  [local(): pl.pallas_call(body, name=name, out_shape=tuple((jax.ShapeDtypeStruct(s,...]
    pallas_call x2 -> x0, other arithmetic: 1.24 us -> none  [exchange(): pl.pallas_call(swap_kernel, name='swap', out_shape=tuple((jax.ShapeDtypeS...]
where the time goes in v5:
time: 89.8 us; the launch traced here: 89.6 us
  Pallas kernels  87.2 us (97%)
  local copies, waits for them, and re-layouts  1.78 us (2%)
    pallas_call x1, Pallas kernels, exchange(): pl.pallas_call(swap_kernel, name='swap', out_shape=tuple((jax.ShapeDtypeS...  77.7 us
    pallas_call x2, Pallas kernels, local(): pl.pallas_call(body, name=name, out_shape=tuple((jax.ShapeDtypeStruct(s,...  9.45 us

profile of v5, /device:TPU:1, one launch (start us, length us, event | category | flops | bytes accessed | tf_op | source)
XLA Modules:
  0.0 89.6 jit_solution(10775072048415458584)
XLA Ops:
  0.6 0.0 copy-start
  0.6 0.0 copy-start.1
  0.7 6.1 %pack.1 = (bf16[128,16,512]{2,1,0:T(8,128)(2,1)S(1)}, bf16[128,2,256]{2,1,0:T(2,128)(2,1)S(1)}, s32[1,128]{1,0:T(1,128)S(1)}, f32[4,16,1,512]{3,2,1,0:T(1,128)S(1)}, f32[1,384]{1,0:T(1,128)S(1)}) custom-call(bf16[2048,256]{1,0:T(8,128)(2,1)} %k_ref.1, bf16[2048,256]{1,0:T(8,128)(2,1)} %v_ref.1, s32[16,128]{1,0:T(8,128)} %bitcast.7, s32[16,128]{1,0:T(8,128)} %bitcast.8, ...), custom_call_target="tpu_custom_call" | custom-call | tf_op jit(solution)/shard_map/pack/pallas_call | solution.py:428
  6.8 0.0 copy-done
  6.8 0.0 copy-done.1
  6.8 77.7 %swap.1 = (bf16[64,16,512]{2,1,0:T(8,128)(2,1)S(1)}, bf16[64,2,256]{2,1,0:T(2,128)(2,1)S(1)}, bf16[6,32]{1,0:T(8,128)(2,1)S(1)}, bf16[1040]{0:T(1024)(128)(2,1)S...) custom-call(s32[1,128]{1,0:T(1,128)S(1)} %get-tuple-element.19.counts, ...), custom_call_target="tpu_custom_call" | custom-call | tf_op jit(solution)/shard_map/swap/pallas_call | solution.py:406
  84.5 3.3 %place.1 = (bf16[1040,256]{1,0:T(8,128)(2,1)}, bf16[1040,256]{1,0:T(8,128)(2,1)}) custom-call(bf16[64,16,512]{2,1,0:T(8,128)(2,1)S(1)} %get-tuple-element.24.recv, bf16[64,2,256]{2,1,0:T(2,128)(2,1)S(1)} %get-tuple-element.25.xrecv, s32[1,1024]{1,0:T(1,128)S(1)} %get-tuple-element.26.tgt, s32[1,128]{1,0:T(1,128)S(1)} %get-tuple-element.27.xtgt), custom_call_target="tpu_custom_call" | custom-call | tf_op jit(solution)/shard_map/place/pallas_call | solution.py:428
  87.9 0.6 copy.17
  88.4 0.6 copy.18
  89.0 0.6 copy.19
Async XLA Ops:
  0.6 6.1 %copy-start = (bf16[256,32]{0,1:T(8,128)(2,1)S(1)}, bf16[256,32]{0,1:T(8,128)(2,1)}, u32[]{:S(2)}) copy-start(bf16[256,32]{0,1:T(8,128)(2,1)} %param.17) | copy-start | bytes 49156
  0.6 6.1 %copy-start.1 = (s32[48]{0:T(128)S(1)}, s32[48]{0:T(128)}, u32[]{:S(2)}) copy-start(s32[48]{0:T(128)} %param.13) | copy-start | bytes 580
